TPU v7x, 256 devices: a whole 4x4x8 slice. The times are simulated.
256 devices in a mesh: dp: 16 (over x, y), rows: 16 (over z, core).
Axes of the slice: x: 4, y: 4, z: 8, core: 2. Of those that a mesh axis runs over, the one named last changes fastest.
Arguments:
- scenes: bfloat16 [16, 256, 256, 384], P('dp', 'rows'), may hold values from -6 to 6
- prompt: bfloat16 [256, 256, 384], P('rows'), may hold values from -6 to 6
- cotangent: bfloat16 [16, 256, 256, 384], P('dp', 'rows'), may hold values from -6 to 6
- first_weight: bfloat16 [2, 8, 48, 48], replicated, may hold values from -0.625 to 0.625
- first_bias: float32 [2, 384], replicated, may hold values from -3 to 3
- second_weight: bfloat16 [2, 8, 48, 48], replicated, may hold values from -0.625 to 0.625
- second_bias: float32 [2, 384], replicated, may hold values from -3 to 3
Outputs:
- mixed: bfloat16 [16, 256, 256, 384], P('dp', 'rows')
- prompt_grad: float32 [256, 256, 384], P('rows', 'dp')
All inputs are finite; a program needn't handle non-finite values.
Results may differ from a plain program's by a relative error of at most 0.014.
Values may be sent and summed in bfloat16 or wider, within the bound.
No kernel may reach another device: no remote copies, remote signals or barrier semaphores. Data moves between devices by JAX's collectives and lax.ppermute only.
A program may use at most 128 MiB of HBM per device.

v0:
```python
import math

import jax
import jax.numpy as jnp
from jax import lax
from jax.sharding import PartitionSpec as P

H = 256
W = 256
NB = 8
BS = 48
KW = 128


def product(form, left, right):
    return jnp.einsum(form, left, right, preferred_element_type=jnp.float32)


def row_tables():
    grid_index = jnp.arange(W, dtype=jnp.int32)
    mode_index = jnp.arange(KW, dtype=jnp.int32)
    phases = mode_index[:, None] * grid_index[None, :] % W
    angles = phases.astype(jnp.float32) * (2.0 * math.pi / W)
    factor = 1.0 / math.sqrt(W)
    cosine = jnp.cos(angles) * factor
    sines = jnp.sin(angles) * factor
    forward = jnp.stack([cosine, -sines], axis=0).astype(jnp.bfloat16)
    doubled = jnp.where(mode_index == 0, 1.0, 2.0).astype(jnp.float32)[:, None]
    inverse = jnp.stack([doubled * cosine, -doubled * sines], axis=0).astype(jnp.bfloat16)
    return (forward, jnp.transpose(inverse, (2, 0, 1)))


def column_tables():
    grid_index = jnp.arange(H, dtype=jnp.int32)
    phases = grid_index[:, None] * grid_index[None, :] % H
    angles = phases.astype(jnp.float32) * (2.0 * math.pi / H)
    factor = 1.0 / math.sqrt(H)
    cosine = jnp.cos(angles) * factor
    sines = jnp.sin(angles) * factor
    upper = jnp.stack([cosine, sines], axis=1)
    lower = jnp.stack([-sines, cosine], axis=1)
    forward = jnp.stack([upper, lower], axis=0).astype(jnp.bfloat16)
    return (forward, jnp.transpose(forward, (2, 3, 0, 1)))


def complex_block(weights):
    real_part = weights[0]
    imag_part = weights[1]
    first_row = jnp.stack([real_part, imag_part], axis=2)
    second_row = jnp.stack([-imag_part, real_part], axis=2)
    return jnp.stack([first_row, second_row], axis=0)


def spectral_mix(spectrum, first_block, second_block, first_bias, second_bias):
    layout = spectrum.shape
    pieces = spectrum.reshape(layout[:4] + (NB, BS))
    first_pre = product("smqkbi,qbipj->smpkbj", pieces, first_block) + first_bias.reshape(
        2, 1, NB, BS
    )
    hidden = jax.nn.gelu(first_pre, approximate=False).astype(jnp.bfloat16)
    second = product("smqkbi,qbipj->smpkbj", hidden, second_block) + second_bias.reshape(
        2, 1, NB, BS
    )
    return (second.astype(jnp.bfloat16).reshape(layout), first_pre)


def spectral_back(back_out, first_pre, first_block, second_block):
    layout = back_out.shape
    pieces = back_out.reshape(layout[:4] + (NB, BS))
    back_hidden = product("smpkbj,qbipj->smqkbi", pieces, second_block)
    cumulative = 0.5 * (1.0 + lax.erf(first_pre * 0.7071067811865476))
    density = jnp.exp(-0.5 * first_pre * first_pre) * 0.3989422804014327
    back_pre = (back_hidden * (cumulative + first_pre * density)).astype(jnp.bfloat16)
    back_spectrum = product("smpkbj,qbipj->smqkbi", back_pre, first_block)
    return back_spectrum.astype(jnp.bfloat16).reshape(layout)


def on_device(scenes, prompt, cotangent, first_weight, first_bias, second_weight, second_bias):
    row_fwd, row_inv = row_tables()
    column_fwd, column_inv = column_tables()
    first_block = complex_block(first_weight)
    second_block = complex_block(second_weight)
    summed = (scenes.astype(jnp.float32) + prompt.astype(jnp.float32)[None]).astype(jnp.bfloat16)
    row_spec = product("pkn,shnc->shpkc", row_fwd, summed).astype(jnp.bfloat16)
    back_spec = product("npk,shnc->shpkc", row_inv, cotangent).astype(jnp.bfloat16)
    row_cols = lax.all_to_all(row_spec, "rows", split_axis=3, concat_axis=1, tiled=True)
    spectrum = product("pmqh,shqkc->smpkc", column_fwd, row_cols).astype(jnp.bfloat16)
    output_spec, first_pre = spectral_mix(
        spectrum, first_block, second_block, first_bias, second_bias
    )
    grid_cols = product("phqm,smqkc->shpkc", column_inv, output_spec).astype(jnp.bfloat16)
    grid_spec = lax.all_to_all(grid_cols, "rows", split_axis=1, concat_axis=3, tiled=True)
    back_cols = lax.all_to_all(back_spec, "rows", split_axis=3, concat_axis=1, tiled=True)
    back_out = product("qhpm,shqkc->smpkc", column_inv, back_cols).astype(jnp.bfloat16)
    back_spectrum = spectral_back(back_out, first_pre, first_block, second_block)
    grad_cols = product("pmqh,smpkc->shqkc", column_fwd, back_spectrum).astype(jnp.bfloat16)
    back_rows = lax.all_to_all(grad_cols, "rows", split_axis=1, concat_axis=3, tiled=True)
    mixed = (summed.astype(jnp.float32) + product("npk,shpkc->shnc", row_inv, grid_spec)).astype(
        jnp.bfloat16
    )
    grad_terms = cotangent.astype(jnp.float32) + product("pkn,shpkc->shnc", row_fwd, back_rows)
    local_grad = jnp.sum(grad_terms, axis=0)
    prompt_grad = lax.psum_scatter(
        local_grad.astype(jnp.bfloat16), "dp", scatter_dimension=1, tiled=True
    ).astype(jnp.float32)
    return (mixed, prompt_grad)


def solution(mesh):
    return jax.shard_map(
        on_device,
        mesh=mesh,
        in_specs=(
            P("dp", "rows", None, None),
            P("rows", None, None),
            P("dp", "rows", None, None),
            P(),
            P(),
            P(),
            P(),
        ),
        out_specs=(P("dp", "rows", None, None), P("rows", "dp", None)),
        check_vma=False,
    )
```

profile of v0, /device:TPU:2, one launch (start us, length us, event | category | flops | bytes accessed | tf_op | source)
XLA Modules:
  0.0 394.9 jit_solution(7331285162131553039)
XLA Ops:
  7.2 0.5 negate_convert_fusion.1
  7.7 3.2 copy.116
  11.0 5.4 %copy.117 = bf16[16,256,384]{1,2,0:T(8,128)(2,1)} copy(bf16[16,256,384]{2,1,0:T(8,128)(2,1)} %param.8) | data formatting | bytes 6291456 | tf_op args[1]
  16.4 4.6 %convert_bitcast_fusion.1 = bf16[1,16,2,128,384]{3,4,2,1,0:T(8,128)(2,1)} fusion(bf16[1,16,256,384]{2,3,1,0:T(8,128)(2,1)S(1)} %copy.116, bf16[16,256,384]{1,2,0:T(8,128)(2,1)} %copy.117, bf16[1,128,256]{2,1,0:T(8,128)(2,1)S(1)} %get-tuple-element.22, bf16[1,128,256]{2,1,0:T(8,128)(2,1)S(1)} %get-tuple-element.23), kind=kOutput, calls=%fused_computation.73 | convolution fusion | flops 813432832 | bytes 9568256 | tf_op jit(solution)/shard_map/pkn,shnc->shpkc/dot_general | solution.py:16
  21.0 8.9 %copy.124 = bf16[1,16,2,128,384]{4,2,1,0,3:T(2,128)(2,1)} copy(bf16[1,16,2,128,384]{3,4,2,1,0:T(8,128)(2,1)} %convert_bitcast_fusion.1) | data formatting | bytes 6291456 | tf_op jit(solution)/shard_map/convert_element_type | solution.py:84
  29.9 8.6 %all-to-all-start = ((bf16[1,16,2,128,384]{4,2,1,0,3:T(2,128)(2,1)}), bf16[1,16,2,128,384]{4,2,1,0,3:T(2,128)(2,1)}, u32[]{:S(2)}, u32[]{:S(2)}) async-start(bf16[1,16,2,128,384]{4,2,1,0,3:T(2,128)(2,1)} %copy.124), calls=%async_computation | async-start | bytes 6291456 | tf_op jit(solution)/shard_map/all_to_all | solution.py:86
  38.6 0.5 multiply_convert_fusion.1
  39.1 0.6 copy-done.14
  39.7 0.0 copy-done.16
  39.8 1.0 convert_bitcast_fusion
  40.8 0.0 copy-start.26
  40.8 3.5 copy.141
  44.3 66.1 %all-to-all-done = bf16[1,16,2,128,384]{4,2,1,0,3:T(2,128)(2,1)} async-done(((bf16[1,16,2,128,384]{4,2,1,0,3:T(2,128)(2,1)}), bf16[1,16,2,128,384]{4,2,1,0,3:T(2,128)(2,1)}, u32[]{:S(2)}, u32[]{:S(2)}) %all-to-all-start) | async-done | bytes 3145760 | tf_op jit(solution)/shard_map/all_to_all | solution.py:86
  110.4 4.7 %all-to-all-start.2 = ((bf16[1,16,2,128,384]{4,1,2,0,3:T(8,128)(2,1)}), bf16[1,16,2,128,384]{4,1,2,0,3:T(8,128)(2,1)}, u32[]{:S(2)}, u32[]{:S(2)}) async-start(bf16[1,16,2,128,384]{4,1,2,0,3:T(8,128)(2,1)} %copy.141), calls=%async_computation.2 | async-start | bytes 6291456 | tf_op jit(solution)/shard_map/all_to_all | solution.py:93
  115.1 1.0 fusion.112
  116.1 0.1 copy.216
  116.2 0.7 copy.215
  116.9 1.0 fusion.111
  117.9 0.7 copy.214
  118.7 0.7 copy.213
  119.4 0.1 add.98
  119.5 1.0 fusion.91
  120.5 1.1 negate_convert_fusion
  121.6 1.1 maximum_bitcast_fusion.4
  122.7 0.9 bitcast_negate_fusion.1
  123.6 1.8 maximum_bitcast_fusion.2
  125.5 1.1 pad_maximum_fusion
  126.6 3.0 copy.272
  129.6 0.5 copy.126
  130.1 3.7 bitcast_convert_fusion.4
  133.9 53.0 %all-to-all-done.2 = bf16[1,16,2,128,384]{4,1,2,0,3:T(8,128)(2,1)} async-done(((bf16[1,16,2,128,384]{4,1,2,0,3:T(8,128)(2,1)}), bf16[1,16,2,128,384]{4,1,2,0,3:T(8,128)(2,1)}, u32[]{:S(2)}, u32[]{:S(2)}) %all-to-all-start.2) | async-done | bytes 3145760 | tf_op jit(solution)/shard_map/all_to_all | solution.py:93
  186.9 3.1 copy.271
  190.0 0.5 copy.143
  190.5 2.1 bitcast_convert_fusion.2
  192.6 1.0 fusion.44
  193.7 3.8 fusion.51
  197.5 1.0 fusion.21
  198.6 0.3 copy.150
  198.9 3.5 fusion.22
  202.4 8.8 %copy.153 = bf16[1,256,2,8,384]{4,2,3,0,1:T(2,128)(2,1)} copy(bf16[1,256,2,8,384]{1,4,2,3,0:T(8,128)(2,1)} %fusion.22) | data formatting | bytes 6291456 | tf_op jit(solution)/shard_map/convert_element_type | solution.py:96
  211.2 4.8 %all-to-all-start.3 = ((bf16[1,256,2,8,384]{4,2,3,0,1:T(2,128)(2,1)}), bf16[1,256,2,8,384]{4,2,3,0,1:T(2,128)(2,1)}, u32[]{:S(2)}, u32[]{:S(2)}) async-start(bf16[1,256,2,8,384]{4,2,3,0,1:T(2,128)(2,1)} %copy.153), calls=%async_computation.3 | async-start | bytes 6291456 | tf_op jit(solution)/shard_map/all_to_all | solution.py:97
  216.0 2.9 copy.140
  218.9 0.1 add.101
  219.0 16.9 %fusion.11 = bf16[1,256,2,8,8,48]{1,5,3,2,4,0:T(8,128)(2,1)S(1)} fusion(f32[2,8,48]{2,0,1:T(2,128)S(1)} %copy.131, bf16[1,8,48,2,48]{2,4,0,3,1:T(8,128)(2,1)S(1)} %copy-done.25, bf16[1,8,48,2,48]{2,4,0,3,1:T(8,128)(2,1)S(1)} %copy-done.23, f32[2,8,48]{2,0,1:T(2,128)S(1)} %copy.129, f32[8,2,48,256,8,1]{3,2,5,4,1,0:T(8,128)} %copy-done), kind=kOutput, calls=%fused_computation.16 | convolution fusion | flops 409239552 | bytes 9590784 | tf_op jit(solution)/shard_map/smqkbi,qbipj->smpkbj/dot_general | solution.py:16
  236.0 0.3 copy.132
  236.3 0.7 copy-done.12
  237.0 1.8 fusion.20
  238.8 6.0 %copy.135 = bf16[1,256,2,8,384]{4,2,3,0,1:T(2,128)(2,1)} copy(bf16[1,256,2,8,384]{1,4,2,3,0:T(8,128)(2,1)S(1)} %fusion.20) | data formatting | bytes 6291456 | tf_op jit(solution)/shard_map/convert_element_type | solution.py:91
  244.8 43.0 %all-to-all-done.3 = bf16[1,256,2,8,384]{4,2,3,0,1:T(2,128)(2,1)} async-done(((bf16[1,256,2,8,384]{4,2,3,0,1:T(2,128)(2,1)}), bf16[1,256,2,8,384]{4,2,3,0,1:T(2,128)(2,1)}, u32[]{:S(2)}, u32[]{:S(2)}) %all-to-all-start.3) | async-done | bytes 3145760 | tf_op jit(solution)/shard_map/all_to_all | solution.py:97
  287.8 4.6 %all-to-all-start.1 = ((bf16[1,256,2,8,384]{4,2,3,0,1:T(2,128)(2,1)}), bf16[1,256,2,8,384]{4,2,3,0,1:T(2,128)(2,1)S(1)}, u32[]{:S(2)}, u32[]{:S(2)}) async-start(bf16[1,256,2,8,384]{4,2,3,0,1:T(2,128)(2,1)} %copy.135), calls=%async_computation.1 | async-start | bytes 6291456 | tf_op jit(solution)/shard_map/all_to_all | solution.py:92
  292.4 0.0 reduce-scatter.2.cloned.1.call-start
  292.5 2.7 copy.154
  295.2 0.1 copy-done.6
  295.3 2.8 fusion.23
  298.1 5.1 %copy.157 = bf16[16,256,384]{2,0,1:T(8,128)(2,1)} copy(bf16[16,256,384]{1,2,0:T(8,128)(2,1)} %fusion.23) | data formatting | bytes 6291456 | tf_op jit(solution)/shard_map/convert_element_type | solution.py:104
  303.2 0.0 reduce-scatter.2.cloned.1.call-update
  303.2 61.0 %all-to-all-done.1 = bf16[1,256,2,8,384]{4,2,3,0,1:T(2,128)(2,1)S(1)} async-done(((bf16[1,256,2,8,384]{4,2,3,0,1:T(2,128)(2,1)}), bf16[1,256,2,8,384]{4,2,3,0,1:T(2,128)(2,1)S(1)}, u32[]{:S(2)}, u32[]{:S(2)}) %all-to-all-start.1) | async-done | bytes 3145760 | tf_op jit(solution)/shard_map/all_to_all | solution.py:92
  364.2 0.6 copy.136
  364.9 1.2 copy-done.3
  366.1 1.0 copy-done.4
  367.1 1.6 fusion.10
  368.6 2.8 copy.158
  371.4 14.9 %reduce-scatter.2.cloned.1.call-done = bf16[16,16,384]{2,0,1:T(8,128)(2,1)} async-done(((bf16[16,256,384]{2,0,1:T(8,128)(2,1)}), bf16[16,16,384]{2,0,1:T(8,128)(2,1)}) %reduce-scatter.2.cloned.1.call-update) | async-done | bytes 196624 | tf_op jit(solution)/shard_map/reduce_scatter | solution.py:103
  386.3 1.7 copy.159
  (55 shorter events, 0.2 us)
Async XLA Ops:
  7.7 8.7 %copy-start.18 = (bf16[1,128,256]{2,1,0:T(8,128)(2,1)}, bf16[1,128,256]{2,1,0:T(8,128)(2,1)S(1)}, u32[]{:S(2)}) copy-start(bf16[1,128,256]{2,1,0:T(8,128)(2,1)S(1)} %get-tuple-element.22) | copy-start | bytes 196612
  7.7 8.7 %copy-start.20 = (bf16[1,128,256]{2,1,0:T(8,128)(2,1)}, bf16[1,128,256]{2,1,0:T(8,128)(2,1)S(1)}, u32[]{:S(2)}) copy-start(bf16[1,128,256]{2,1,0:T(8,128)(2,1)S(1)} %get-tuple-element.23) | copy-start | bytes 196612
  11.0 5.4 %copy-start.2 = (bf16[1,16,256,384]{2,3,1,0:T(8,128)(2,1)}, bf16[1,16,256,384]{2,3,1,0:T(8,128)(2,1)S(1)}, u32[]{:S(2)}) copy-start(bf16[1,16,256,384]{2,3,1,0:T(8,128)(2,1)S(1)} %copy.116) | copy-start | bytes 9437188
  21.0 18.7 %copy-start.1 = (bf16[1,16,256,384]{3,2,1,0:T(8,128)(2,1)S(1)}, bf16[1,16,256,384]{3,2,1,0:T(8,128)(2,1)}, u32[]{:S(2)}) copy-start(bf16[1,16,256,384]{3,2,1,0:T(8,128)(2,1)} %param.9) | copy-start | bytes 9437188
  29.9 80.5 %all-to-all-start = ((bf16[1,16,2,128,384]{4,2,1,0,3:T(2,128)(2,1)}), bf16[1,16,2,128,384]{4,2,1,0,3:T(2,128)(2,1)}, u32[]{:S(2)}, u32[]{:S(2)}) async-start(bf16[1,16,2,128,384]{4,2,1,0,3:T(2,128)(2,1)} %copy.124), calls=%async_computation | async-start | bytes 6291456 | tf_op jit(solution)/shard_map/all_to_all | solution.py:86
  39.1 0.6 copy-start.14
  39.1 0.6 copy-start.16
  40.8 78.6 %copy-start.26 = (f32[2,384]{1,0:T(2,128)S(1)}, f32[2,384]{1,0:T(2,128)}, u32[]{:S(2)}) copy-start(f32[2,384]{1,0:T(2,128)} %param.11) | copy-start | bytes 9220
  110.4 76.5 %all-to-all-start.2 = ((bf16[1,16,2,128,384]{4,1,2,0,3:T(8,128)(2,1)}), bf16[1,16,2,128,384]{4,1,2,0,3:T(8,128)(2,1)}, u32[]{:S(2)}, u32[]{:S(2)}) async-start(bf16[1,16,2,128,384]{4,1,2,0,3:T(8,128)(2,1)} %copy.141), calls=%async_computation.2 | async-start | bytes 6291456 | tf_op jit(solution)/shard_map/all_to_all | solution.py:93
  116.2 5.4 %copy-start.11 = (bf16[1,8,48,48]{2,3,1,0:T(8,128)(2,1)}, bf16[1,8,48,48]{2,3,1,0:T(8,128)(2,1)S(1)}, u32[]{:S(2)}) copy-start(bf16[1,8,48,48]{2,3,1,0:T(8,128)(2,1)S(1)} %copy.216) | copy-start | bytes 110596
  125.5 4.6 %copy-start.7 = (bf16[1,256,2,256]{3,1,2,0:T(8,128)(2,1)}, bf16[1,256,2,256]{3,1,2,0:T(8,128)(2,1)S(1)}, u32[]{:S(2)}) copy-start(bf16[1,256,2,256]{3,1,2,0:T(8,128)(2,1)S(1)} %get-tuple-element.16) | copy-start | bytes 786436
  125.5 4.6 %copy-start.9 = (bf16[1,256,2,256]{3,1,2,0:T(8,128)(2,1)}, bf16[1,256,2,256]{3,1,2,0:T(8,128)(2,1)S(1)}, u32[]{:S(2)}) copy-start(bf16[1,256,2,256]{3,1,2,0:T(8,128)(2,1)S(1)} %get-tuple-element.17) | copy-start | bytes 786436
  186.9 3.6 copy-start.8
  186.9 3.6 copy-start.10
  190.5 2.1 copy-start.5
  192.6 1.1 copy-start.22
  192.6 1.1 copy-start.24
  193.7 3.9 copy-start
  197.5 1.3 copy-start.13
  211.2 7.7 %copy-start.27 = (f32[2,384]{1,0:T(2,128)S(1)}, f32[2,384]{1,0:T(2,128)}, u32[]{:S(2)}) copy-start(f32[2,384]{1,0:T(2,128)} %param.13) | copy-start | bytes 9220
  211.2 7.8 %copy-start.23 = (bf16[1,8,48,2,48]{2,4,0,3,1:T(8,128)(2,1)S(1)}, bf16[1,8,48,2,48]{2,4,0,3,1:T(8,128)(2,1)}, u32[]{:S(2)}) copy-start(bf16[1,8,48,2,48]{2,4,0,3,1:T(8,128)(2,1)} %get-tuple-element.18) | copy-start | bytes 221188
  211.2 7.8 %copy-start.25 = (bf16[1,8,48,2,48]{2,4,0,3,1:T(8,128)(2,1)S(1)}, bf16[1,8,48,2,48]{2,4,0,3,1:T(8,128)(2,1)}, u32[]{:S(2)}) copy-start(bf16[1,8,48,2,48]{2,4,0,3,1:T(8,128)(2,1)} %get-tuple-element.19) | copy-start | bytes 221188
  211.2 76.6 %all-to-all-start.3 = ((bf16[1,256,2,8,384]{4,2,3,0,1:T(2,128)(2,1)}), bf16[1,256,2,8,384]{4,2,3,0,1:T(2,128)(2,1)}, u32[]{:S(2)}, u32[]{:S(2)}) async-start(bf16[1,256,2,8,384]{4,2,3,0,1:T(2,128)(2,1)} %copy.153), calls=%async_computation.3 | async-start | bytes 6291456 | tf_op jit(solution)/shard_map/all_to_all | solution.py:97
  235.9 1.0 copy-start.12
  244.8 50.3 %copy-start.19 = (bf16[1,128,256]{2,1,0:T(8,128)(2,1)S(1)}, bf16[1,128,256]{2,1,0:T(8,128)(2,1)}, u32[]{:S(2)}) copy-start(bf16[1,128,256]{2,1,0:T(8,128)(2,1)} %copy-done.18) | copy-start | bytes 196612
  244.8 50.4 %copy-start.21 = (bf16[1,128,256]{2,1,0:T(8,128)(2,1)S(1)}, bf16[1,128,256]{2,1,0:T(8,128)(2,1)}, u32[]{:S(2)}) copy-start(bf16[1,128,256]{2,1,0:T(8,128)(2,1)} %copy-done.20) | copy-start | bytes 196612
  287.8 76.4 %all-to-all-start.1 = ((bf16[1,256,2,8,384]{4,2,3,0,1:T(2,128)(2,1)}), bf16[1,256,2,8,384]{4,2,3,0,1:T(2,128)(2,1)S(1)}, u32[]{:S(2)}, u32[]{:S(2)}) async-start(bf16[1,256,2,8,384]{4,2,3,0,1:T(2,128)(2,1)} %copy.135), calls=%async_computation.1 | async-start | bytes 6291456 | tf_op jit(solution)/shard_map/all_to_all | solution.py:92
  292.4 93.9 %reduce-scatter.2.cloned.1.call-start = ((), (), s32[]{:S(2)}) async-start(), calls=%async_computation.5 | async-start | bytes 3342336 | tf_op jit(solution)/shard_map/reduce_scatter | solution.py:103
  292.5 2.8 copy-start.6
  303.2 61.7 %copy-start.15 = (bf16[1,128,256]{2,1,0:T(8,128)(2,1)S(1)}, bf16[1,128,256]{2,1,0:T(8,128)(2,1)}, u32[]{:S(2)}) copy-start(bf16[1,128,256]{2,1,0:T(8,128)(2,1)} %copy-done.14) | copy-start | bytes 196612
  303.2 61.7 %copy-start.17 = (bf16[1,128,256]{2,1,0:T(8,128)(2,1)S(1)}, bf16[1,128,256]{2,1,0:T(8,128)(2,1)}, u32[]{:S(2)}) copy-start(bf16[1,128,256]{2,1,0:T(8,128)(2,1)} %copy-done.16) | copy-start | bytes 196612
  364.2 1.9 copy-start.3
  364.2 2.8 copy-start.4
Sparse Core Ops, SparseCore 0:
  303.3 82.9 reduce-scatter.1
where the time goes:
time: 396 us; the launch traced here: 395 us
  waiting for transfers between devices  238 us (60%)
  local copies, waits for them, and re-layouts  67.6 us (17%)
  matrix products  43.8 us (11%)
  starting transfers between devices  22.7 us (6%)
  between operations  14.5 us (4%)
  other arithmetic  8.18 us (2%)
    all_to_all x1, waiting for transfers between devices, on_device(): lax.all_to_all(row_spec, 'rows', split_axis=3, concat_axis=1, tiled=True)  66.1 us
    all_to_all x1, waiting for transfers between devices, on_device(): lax.all_to_all(grid_cols, 'rows', split_axis=1, concat_axis=3, tiled=True)  61 us
    all_to_all x1, waiting for transfers between devices, on_device(): lax.all_to_all(back_spec, 'rows', split_axis=3, concat_axis=1, tiled=True)  53 us
    dot_general x12, matrix products, product(): return jnp.einsum(form, left, right, preferred_element_type=jnp.float32)  43.8 us
    all_to_all x1, waiting for transfers between devices, on_device(): lax.all_to_all(grad_cols, 'rows', split_axis=1, concat_axis=3, tiled=True)  43 us
    unnamed x65, local copies, waits for them, and re-layouts  22.1 us
    reduce_scatter x1, waiting for transfers between devices, on_device(): lax.psum_scatter(local_grad.astype(jnp.bfloat16), 'dp', scatter_dimension...  14.9 us
    convert_element_type x1, local copies, waits for them, and re-layouts, on_device(): row_spec = product('pkn,shnc->shpkc', row_fwd, summed).astype(jnp.bfloat16)  8.87 us
  transfers between devices with their start and end apart: 5, of which 5 were waited for; matrix products, arithmetic and copies ran while one was open for 17% of the time, Pallas kernels for 0%

commit v1 on v0

v1 whole, which is shorter than its diff:
```python
import math

import jax
import jax.numpy as jnp
import numpy as np
from jax import lax
from jax.experimental import pallas as pl
from jax.experimental.pallas import tpu as pltpu
from jax.sharding import PartitionSpec as P


H = 256
W = 256
C = 384
NB = 8
BS = 48
KW = 128
N = 16
K8 = 8
BF = jnp.bfloat16
F32 = jnp.float32


def tables():
    grid = np.arange(W)
    modes = np.arange(KW)
    angles = ((modes[:, None] * grid[None, :]) % W).astype(np.float32) * np.float32(2.0 * math.pi / W)
    cosine = np.cos(angles) / np.float32(16.0)
    sine = np.sin(angles) / np.float32(16.0)
    forward = np.stack([cosine, -sine])
    doubled = np.where(modes == 0, 1.0, 2.0).astype(np.float32)[:, None]
    inverse = np.stack([doubled * cosine, -doubled * sine])

    def by_owner(table):
        return table.reshape(2, N, K8, W).transpose(1, 0, 2, 3).reshape(W, W).astype(BF)

    row_fwd, row_inv = by_owner(forward), by_owner(inverse)
    angles = ((grid[:, None] * grid[None, :]) % H).astype(np.float32) * np.float32(2.0 * math.pi / H)
    c = np.cos(angles) / np.float32(16.0)
    s = np.sin(angles) / np.float32(16.0)
    return row_fwd, row_inv, np.stack([c, s]).astype(BF)


ROW_FWD, ROW_INV, COL = tables()
TILE = (np.arange(C)[None, :] % BS == np.arange(BS)[:, None]).astype(BF)
BLOCK_OF = (np.arange(C)[:, None] // BS == np.arange(NB)[None, :]).astype(BF)


def dot(a, b):
    return jnp.dot(a, b, preferred_element_type=F32)


def cost(flops, bytes_accessed):
    return pl.CostEstimate(flops=int(flops), bytes_accessed=int(bytes_accessed), transcendentals=0)


def full(shape):
    return pl.BlockSpec(shape, lambda i: (0,) * len(shape))


HB = 2


def rows_scene_kernel(table, scene, prompt, out):
    for i in range(HB):
        summed = (scene[i].astype(F32) + prompt[i].astype(F32)).astype(BF)
        out[:, i] = dot(table[...], summed).astype(BF).reshape(N, 16, C)


def rows_cot_kernel(table, cot, out, pieces):
    for i in range(HB):
        x = cot[i]
        out[:, i] = dot(table[...], x).astype(BF).reshape(N, 16, C)
        pieces[:, i] = x.reshape(N, 16, C)


GRID_SPEC = pl.BlockSpec((HB, W, C), lambda i: (i, 0, 0))
SPEC_SPEC = pl.BlockSpec((N, HB, 16, C), lambda i: (0, i, 0, 0))
SPEC_SHAPE = jax.ShapeDtypeStruct((N, N, 16, C), BF)
ROW_FLOPS = 2 * 256 * 256 * N * C
ARRAY_BYTES = 2 * N * W * C


def rows_scene(scene, prompt):
    return pl.pallas_call(
        rows_scene_kernel,
        grid=(N // HB,),
        in_specs=[full((W, W)), GRID_SPEC, GRID_SPEC],
        out_specs=SPEC_SPEC,
        out_shape=SPEC_SHAPE,
        cost_estimate=cost(ROW_FLOPS, 3 * ARRAY_BYTES),
        name="rows_scene",
    )(ROW_FWD, scene, prompt)


def rows_cot(cot):
    return pl.pallas_call(
        rows_cot_kernel,
        grid=(N // HB,),
        in_specs=[full((W, W)), GRID_SPEC],
        out_specs=[SPEC_SPEC, SPEC_SPEC],
        out_shape=[SPEC_SHAPE, SPEC_SHAPE],
        cost_estimate=cost(ROW_FLOPS, 3 * ARRAY_BYTES),
        name="rows_cot",
    )(ROW_INV, cot)


LANES = 128
TILES = C // LANES


def load_block(received, wide):
    def step(r, carry):
        rows = received[r].astype(F32).reshape(256, C)
        for t in range(TILES):
            wide[t, pl.ds(pl.multiple_of(r * 256, 256), 256), :] = rows[:, t * LANES : (t + 1) * LANES]
        return carry

    lax.fori_loop(0, N, step, 0)


def block_of(wide, r):
    rows = pl.ds(pl.multiple_of(r * 256, 256), 256)
    return jnp.concatenate([wide[t, rows, :].astype(BF) for t in range(TILES)], axis=1).reshape(N, 16, C)


def columns_of(wide, k):
    halves = []
    for q in range(2):
        rows = pl.ds(q * K8 + k, H, stride=16)
        halves.append(jnp.concatenate([wide[t, rows, :].astype(BF) for t in range(TILES)], axis=1))
    return jnp.concatenate(halves, axis=0)


def store_columns(wide, k, value):
    for q in range(2):
        rows = pl.ds(q * K8 + k, H, stride=16)
        for t in range(TILES):
            wide[t, rows, :] = value[q * H : (q + 1) * H, t * LANES : (t + 1) * LANES]


def to_lanes(rows):
    return jnp.concatenate([rows[:H], rows[H:]], axis=1)


def to_rows(lanes):
    return jnp.concatenate([lanes[:, :C], lanes[:, C:]], axis=0)


def same_block(member):
    return lax.dot_general(member[...], member[...], (((1,), (1,)), ((), ())), preferred_element_type=F32)


def expand(weight, tile, member, dense):
    mask = same_block(member)
    real = (dot(weight[0], tile[...]) * mask).astype(BF)
    imag = (dot(weight[1], tile[...]) * mask).astype(BF)
    dense[:C, :C] = real
    dense[:C, C:] = imag
    dense[C:, :C] = -imag
    dense[C:, C:] = real


def expand_transposed(weight, tile, member, dense):
    mask = same_block(member)

    def spread(part):
        wide = lax.dot_general(tile[...], part, (((0,), (1,)), ((), ())), preferred_element_type=F32)
        return (wide * mask).astype(BF)

    real = spread(weight[0])
    imag = spread(weight[1])
    dense[:C, :C] = real
    dense[:C, C:] = -imag
    dense[C:, :C] = imag
    dense[C:, C:] = real


def mix_kernel(received, col, w1, b1, w2, b2, tile, member, out, slope, wide, dense1, dense2, col_fwd, col_inv):
    k = pl.program_id(0)

    @pl.when(k == 0)
    def _():
        load_block(received, wide)
        column_matrices(col, col_fwd, col_inv)
        expand(w1, tile, member, dense1)
        expand(w2, tile, member, dense2)

    spectrum = dot(col_fwd[...], columns_of(wide, k)).astype(BF)
    bias1 = jnp.concatenate([b1[0:1], b1[1:2]], axis=1)
    bias2 = jnp.concatenate([b2[0:1], b2[1:2]], axis=1)
    z = dot(to_lanes(spectrum), dense1[...]) + bias1
    cumulative = 0.5 * (1.0 + lax.erf(z * 0.7071067811865476))
    hidden = (z * cumulative).astype(BF)
    slope[0] = cumulative + z * (jnp.exp(-0.5 * z * z) * 0.3989422804014327)
    output = (dot(hidden, dense2[...]) + bias2).astype(BF)
    store_columns(wide, k, dot(col_inv[...], to_rows(output)))

    @pl.when(k == K8 - 1)
    def _():
        def step(r, carry):
            out[r] = block_of(wide, r)
            return carry

        lax.fori_loop(0, N, step, 0)


def back_kernel(received, slope, col, w1, w2, tile, member, out, wide, dense1, dense2, col_fwd, col_inv):
    k = pl.program_id(0)

    @pl.when(k == 0)
    def _():
        load_block(received, wide)
        column_matrices(col, col_fwd, col_inv)
        expand_transposed(w1, tile, member, dense1)
        expand_transposed(w2, tile, member, dense2)

    back_out = dot(col_fwd[...], columns_of(wide, k)).astype(BF)
    back_pre = (dot(to_lanes(back_out), dense2[...]) * slope[0]).astype(BF)
    back_spectrum = dot(back_pre, dense1[...]).astype(BF)
    store_columns(wide, k, dot(col_inv[...], to_rows(back_spectrum)))

    @pl.when(k == K8 - 1)
    def _():
        def step(r, carry):
            out[:, r] = block_of(wide, r)
            return carry

        lax.fori_loop(0, N, step, 0)


def column_matrices(col, col_fwd, col_inv):
    c, s = col[0], col[1]
    for matrix, sine in ((col_fwd, s), (col_inv, -s)):
        matrix[:H, :H] = c
        matrix[:H, H:] = sine
        matrix[H:, :H] = -sine
        matrix[H:, H:] = c


MIX_FLOPS = 2 * K8 * (2 * 512 * 512 * C + 2 * 256 * 768 * 768)
MIX_SCRATCH = [
    pltpu.VMEM((TILES, H * 16, LANES), F32),
    pltpu.VMEM((2 * C, 2 * C), BF),
    pltpu.VMEM((2 * C, 2 * C), BF),
    pltpu.VMEM((2 * H, 2 * H), BF),
    pltpu.VMEM((2 * H, 2 * H), BF),
]
SLOPE_SPEC = pl.BlockSpec((1, H, 2 * C), lambda i: (i, 0, 0))
SLOPE_SHAPE = jax.ShapeDtypeStruct((K8, H, 2 * C), F32)
FULL_SPEC = full((N, N, 16, C))


def mix(received, w1, b1, w2, b2):
    return pl.pallas_call(
        mix_kernel,
        grid=(K8,),
        in_specs=[
            FULL_SPEC,
            full((2, H, H)),
            full((2, C, BS)),
            full((2, C)),
            full((2, C, BS)),
            full((2, C)),
            full((BS, C)),
            full((C, NB)),
        ],
        out_specs=[FULL_SPEC, SLOPE_SPEC],
        out_shape=[SPEC_SHAPE, SLOPE_SHAPE],
        scratch_shapes=MIX_SCRATCH,
        cost_estimate=cost(MIX_FLOPS, 4 * ARRAY_BYTES),
        name="mix",
    )(received, COL, w1, b1, w2, b2, TILE, BLOCK_OF)


def back(received, slope, w1, w2):
    return pl.pallas_call(
        back_kernel,
        grid=(K8,),
        in_specs=[
            FULL_SPEC,
            SLOPE_SPEC,
            full((2, H, H)),
            full((2, C, BS)),
            full((2, C, BS)),
            full((BS, C)),
            full((C, NB)),
        ],
        out_specs=FULL_SPEC,
        out_shape=SPEC_SHAPE,
        scratch_shapes=MIX_SCRATCH,
        cost_estimate=cost(MIX_FLOPS, 4 * ARRAY_BYTES),
        name="back",
    )(received, slope, COL, w1, w2, TILE, BLOCK_OF)


def finish_kernel(table, spec, scene, prompt, out):
    for i in range(HB):
        summed = (scene[i].astype(F32) + prompt[i].astype(F32)).astype(BF).astype(F32)
        out[i] = (summed + dot(table[...], spec[:, i].reshape(W, C))).astype(BF)


def finish(spec, scene, prompt):
    return pl.pallas_call(
        finish_kernel,
        grid=(N // HB,),
        in_specs=[full((W, W)), SPEC_SPEC, GRID_SPEC, GRID_SPEC],
        out_specs=GRID_SPEC,
        out_shape=jax.ShapeDtypeStruct((N, W, C), BF),
        cost_estimate=cost(ROW_FLOPS, 4 * ARRAY_BYTES),
        name="finish",
    )(np.ascontiguousarray(ROW_INV.T), spec, scene, prompt)


def grad_row_kernel(table, spec, out):
    out[...] = dot(table[...], spec[...].reshape(W, C)).astype(BF).reshape(N, 16, C)


def grad_row(spec):
    return pl.pallas_call(
        grad_row_kernel,
        grid=(1,),
        in_specs=[full((W, W)), full((N, 16, C))],
        out_specs=full((N, 16, C)),
        out_shape=jax.ShapeDtypeStruct((N, 16, C), BF),
        cost_estimate=cost(ROW_FLOPS // N, 2 * ARRAY_BYTES // N),
        name="grad_row",
    )(np.ascontiguousarray(ROW_FWD.T), spec)


def shifted_sum(parts, axis, mine, perm_of):
    def piece_for(index):
        starts = [jnp.uint32(0)] * parts.ndim
        starts[axis] = index
        sizes = list(parts.shape)
        sizes[axis] = 1
        return lax.squeeze(lax.dynamic_slice(parts, starts, sizes), (axis,))

    total = piece_for(mine).astype(F32)
    for j in (1, 3, 2):
        piece = piece_for((mine + j) & 3)
        total = total + lax.ppermute(piece, "dp", perm_of(j)).astype(F32)
    return total


def along_x(j):
    return [(x * 4 + y, ((x + j) % 4) * 4 + y) for x in range(4) for y in range(4)]


def along_y(j):
    return [(x * 4 + y, x * 4 + (y + j) % 4) for x in range(4) for y in range(4)]


def sum_over_dp(pieces):
    me = lax.axis_index("dp").astype(jnp.uint32)
    x, y = me >> 2, me & 3
    split = pieces.reshape(4, 4, 2, N // 2, 16, C)
    first = shifted_sum(split[:, :, 0], 1, y, along_y).astype(BF)
    second = shifted_sum(split[:, :, 1], 0, x, along_x).astype(BF)
    first = shifted_sum(first, 0, x, along_x)
    second = shifted_sum(second, 0, y, along_y)
    return jnp.concatenate([first, second], axis=0)


def exchange(blocks, axis):
    return lax.all_to_all(blocks, axis, split_axis=0, concat_axis=0, tiled=True)


def on_device(scenes, prompt, cotangent, first_weight, first_bias, second_weight, second_bias):
    scene, cot = scenes[0], cotangent[0]
    w1 = first_weight.reshape(2, C, BS)
    w2 = second_weight.reshape(2, C, BS)
    scene_cols = exchange(rows_scene(scene, prompt), "rows")
    cot_rows, cot_pieces = rows_cot(cot)
    cot_cols = exchange(cot_rows, "rows")
    cot_sum = sum_over_dp(cot_pieces)
    scene_cols, cot_sum = lax.optimization_barrier((scene_cols, cot_sum))
    mixed_cols, slope = mix(scene_cols, w1, first_bias, w2, second_bias)
    mixed_rows = exchange(mixed_cols, "rows")
    grad_sum = sum_over_dp(back(cot_cols, slope, w1, w2)).astype(BF)
    mixed = finish(mixed_rows, scene, prompt)
    grad_rows = exchange(grad_row(exchange(grad_sum, "rows")), "dp")
    prompt_grad = grad_rows.astype(F32) + cot_sum
    return (mixed[None], prompt_grad)


def solution(mesh):
    return jax.shard_map(
        on_device,
        mesh=mesh,
        in_specs=(
            P("dp", "rows", None, None),
            P("rows", None, None),
            P("dp", "rows", None, None),
            P(),
            P(),
            P(),
            P(),
        ),
        out_specs=(P("dp", "rows", None, None), P("rows", "dp", None)),
        check_vma=False,
    )
```

time: 396 us -> 349 us (0.88)
  Pallas kernels: 0 us -> 69.7 us
  waiting for transfers between devices: 238 us -> 169 us
  local copies, waits for them, and re-layouts: 67.6 us -> 9.28 us
  matrix products: 43.8 us -> 0 us
  starting transfers between devices: 22.7 us -> 63.1 us
  blocking collectives: 0 us -> 29.6 us
  between operations: 14.5 us -> 0.83 us
  other arithmetic: 8.18 us -> 4.02 us
    all_to_all x4 -> x3, waiting for transfers between devices: 223 us -> 140 us  [exchange(): return lax.all_to_all(blocks, axis, split_axis=0, concat_axis=0, tiled=True)]
    pallas_call x0 -> x6, Pallas kernels: none -> 69.7 us  [the longest x1 22.5 us: mix(): pl.pallas_call(mix_kernel, grid=(K8,), in_specs=[FULL_SPEC, full((2, H, H...]
    ppermute x0 -> x24, starting transfers between devices: none -> 46.1 us  [shifted_sum(): total = total + lax.ppermute(piece, 'dp', perm_of(j)).astype(F32)]
    dot_general x12 -> x0, matrix products: 43.8 us -> none  [product(): return jnp.einsum(form, left, right, preferred_element_type=jnp.float32)]
    convert_element_type x7 -> x0, local copies, waits for them, and re-layouts: 33 us -> none  [the longest x1 8.87 us: on_device(): row_spec = product('pkn,shnc->shpkc', row_fwd, summed).astype(jnp.bfloat16)]
    all_to_all x0 -> x2, blocking collectives: none -> 29.6 us  [exchange(): return lax.all_to_all(blocks, axis, split_axis=0, concat_axis=0, tiled=True)]
    ppermute x0 -> x24, waiting for transfers between devices: none -> 29.2 us  [shifted_sum(): total = total + lax.ppermute(piece, 'dp', perm_of(j)).astype(F32)]
    unnamed x65 -> x4, local copies, waits for them, and re-layouts: 22.1 us -> 3.31 us
  transfers between devices with their start and end apart: 5 -> 27, of which waited for: 5 -> 12; matrix products, arithmetic and copies ran while one was open for 17% -> 2% of each run, Pallas kernels for 0% -> 9%
where the time goes in v1:
time: 349 us; the launch traced here: 346 us
  waiting for transfers between devices  169 us (48%)
  Pallas kernels  69.7 us (20%)
  starting transfers between devices  63.1 us (18%)
  blocking collectives  29.6 us (8%)
  local copies, waits for them, and re-layouts  9.28 us (3%)
  other arithmetic  4.02 us (1%)
    all_to_all x3, waiting for transfers between devices, exchange(): return lax.all_to_all(blocks, axis, split_axis=0, concat_axis=0, tiled=True)  140 us
    ppermute x24, starting transfers between devices, shifted_sum(): total = total + lax.ppermute(piece, 'dp', perm_of(j)).astype(F32)  46.1 us
    all_to_all x2, blocking collectives, exchange(): return lax.all_to_all(blocks, axis, split_axis=0, concat_axis=0, tiled=True)  29.6 us
    ppermute x24, waiting for transfers between devices, shifted_sum(): total = total + lax.ppermute(piece, 'dp', perm_of(j)).astype(F32)  29.2 us
    pallas_call x1, Pallas kernels, mix(): pl.pallas_call(mix_kernel, grid=(K8,), in_specs=[FULL_SPEC, full((2, H, H...  22.5 us
    pallas_call x1, Pallas kernels, back(): pl.pallas_call(back_kernel, grid=(K8,), in_specs=[FULL_SPEC, SLOPE_SPEC,...  21.6 us
    all_to_all x3, starting transfers between devices, exchange(): return lax.all_to_all(blocks, axis, split_axis=0, concat_axis=0, tiled=True)  17 us
    pallas_call x1, Pallas kernels, finish(): pl.pallas_call(finish_kernel, grid=(N // HB,), in_specs=[full((W, W)), SP...  8.25 us
  transfers between devices with their start and end apart: 27, of which 12 were waited for; matrix products, arithmetic and copies ran while one was open for 2% of the time, Pallas kernels for 9%

profile of v1, /device:TPU:2, one launch (start us, length us, event | category | flops | bytes accessed | tf_op | source)
XLA Modules:
  0.0 345.9 jit_solution(2865760548557695888)
XLA Ops:
  0.6 7.8 %rows_scene.1 = bf16[16,16,16,384]{3,2,1,0:T(8,128)(2,1)} custom-call(bf16[256,256]{1,0:T(8,128)(2,1)} %constant.43.clone.table, bf16[16,256,384]{2,1,0:T(8,128)(2,1)} %bitcast.113, bf16[16,256,384]{2,1,0:T(8,128)(2,1)} %prompt.3), custom_call_target="tpu_custom_call" | custom-call | flops 805306368 | bytes 9437184 | tf_op jit(solution)/shard_map/rows_scene/pallas_call | solution.py:85
  8.4 8.6 %all-to-all-start = ((bf16[16,16,16,384]{3,2,1,0:T(8,128)(2,1)}), bf16[16,16,16,384]{3,2,1,0:T(8,128)(2,1)S(1)}, u32[]{:S(2)}, u32[]{:S(2)}) async-start(bf16[16,16,16,384]{3,2,1,0:T(8,128)(2,1)} %rows_scene.1), calls=%async_computation | async-start | bytes 6291456 | tf_op jit(solution)/shard_map/all_to_all | solution.py:366
  17.0 7.8 %rows_cot.1 = (bf16[16,16,16,384]{3,2,1,0:T(8,128)(2,1)}, bf16[16,16,16,384]{3,2,1,0:T(8,128)(2,1)}) custom-call(bf16[256,256]{1,0:T(8,128)(2,1)} %constant.44.clone.table, bf16[16,256,384]{2,1,0:T(8,128)(2,1)} %bitcast.115), custom_call_target="tpu_custom_call" | custom-call | flops 805306368 | bytes 9437184 | tf_op jit(solution)/shard_map/rows_cot/pallas_call | solution.py:97
  24.7 64.1 %all-to-all-done.received = bf16[16,16,16,384]{3,2,1,0:T(8,128)(2,1)S(1)} async-done(((bf16[16,16,16,384]{3,2,1,0:T(8,128)(2,1)}), bf16[16,16,16,384]{3,2,1,0:T(8,128)(2,1)S(1)}, u32[]{:S(2)}, u32[]{:S(2)}) %all-to-all-start) | async-done | bytes 3145760 | tf_op jit(solution)/shard_map/all_to_all | solution.py:366
  88.8 1.7 copy-done.1
  90.5 4.6 %all-to-all-start.2 = ((bf16[16,16,16,384]{3,2,1,0:T(8,128)(2,1)}), bf16[16,16,16,384]{3,2,1,0:T(8,128)(2,1)}, u32[]{:S(2)}, u32[]{:S(2)}) async-start(bf16[16,16,16,384]{3,2,1,0:T(8,128)(2,1)} %get-tuple-element.11), calls=%async_computation.2 | async-start | bytes 6291456 | tf_op jit(solution)/shard_map/all_to_all | solution.py:366
  95.1 2.2 fusion.23
  97.3 1.0 dynamic-slice_bitcast_fusion.11
  98.3 1.6 collective-permute-start
  99.9 1.7 collective-permute-start.1
  101.6 2.0 collective-permute-start.2
  103.5 0.1 dynamic-slice_bitcast_fusion.8
  103.7 1.6 collective-permute-start.6
  105.2 0.5 collective-permute-start.7
  105.8 5.5 %collective-permute-done = bf16[4,8,16,384]{3,2,1,0:T(8,128)(2,1)} collective-permute-done((bf16[4,8,16,384]{3,2,1,0:T(8,128)(2,1)}, bf16[4,8,16,384]{3,2,1,0:T(8,128)(2,1)}, u32[]{:S(2)}, u32[]{:S(2)}) %collective-permute-start) | collective-permute-done | bytes 393248 | tf_op jit(solution)/shard_map/ppermute | solution.py:342
  111.3 2.1 collective-permute-start.8
  113.4 0.0 collective-permute-done.1
  113.4 7.5 %collective-permute-done.2 = bf16[4,8,16,384]{3,2,1,0:T(8,128)(2,1)} collective-permute-done((bf16[4,8,16,384]{3,2,1,0:T(8,128)(2,1)S(1)}, bf16[4,8,16,384]{3,2,1,0:T(8,128)(2,1)}, u32[]{:S(2)}, u32[]{:S(2)}) %collective-permute-start.2) | collective-permute-done | bytes 393248 | tf_op jit(solution)/shard_map/ppermute | solution.py:342
  120.9 1.4 fusion.11
  122.4 1.6 collective-permute-start.3
  123.9 1.1 collective-permute-start.5
  125.0 0.0 collective-permute-done.6
  125.0 2.2 collective-permute-start.4
  127.2 0.2 fusion.8
  127.4 1.2 collective-permute-start.9
  128.7 4.8 %collective-permute-start.11 = (bf16[8,16,384]{2,1,0:T(8,128)(2,1)S(1)}, bf16[8,16,384]{2,1,0:T(8,128)(2,1)S(1)}, u32[]{:S(2)}, u32[]{:S(2)}) collective-permute-start(bf16[8,16,384]{2,1,0:T(8,128)(2,1)S(1)} %get-tuple-element.40), channel_id=1, source_target_pairs={{0,32},{16,48},{32,0},{48,16},{64,96},{80,112},{96,64},{112,80},{1... | collective-permute-start | bytes 294920 | tf_op jit(solution)/shard_map/ppermute | solution.py:342
  133.5 2.5 collective-permute-start.10
  136.1 0.9 collective-permute-done.11
  137.0 1.2 collective-permute-done.10
  138.3 22.5 %mix.1 = (bf16[16,16,16,384]{3,2,1,0:T(8,128)(2,1)}, f32[8,256,768]{2,1,0:T(8,128)}) custom-call(bf16[16,16,16,384]{3,2,1,0:T(8,128)(2,1)} %copy-done.1, bf16[2,256,256]{2,1,0:T(8,128)(2,1)} %constant.45.clone.col, bf16[2,384,48]{2,1,0:T(8,128)(2,1)} %bitcast.119, f32[2,384]{1,0:T(2,128)} %b1.1, bf16[2,384,48]{2,1,0:T(8,128)(2,1)} %bitcast.121, ...), custom_call_target="tpu_custom_call" | custom-call | flops 8053063680 | bytes 12582912 | tf_op jit(solution)/shard_map/mix/pallas_call | solution.py:255
  160.8 6.2 %all-to-all-done.2.received = bf16[16,16,16,384]{3,2,1,0:T(8,128)(2,1)} async-done(((bf16[16,16,16,384]{3,2,1,0:T(8,128)(2,1)}), bf16[16,16,16,384]{3,2,1,0:T(8,128)(2,1)}, u32[]{:S(2)}, u32[]{:S(2)}) %all-to-all-start.2) | async-done | bytes 3145760 | tf_op jit(solution)/shard_map/all_to_all | solution.py:366
  167.0 21.6 %back.1 = bf16[16,16,16,384]{3,2,1,0:T(8,128)(2,1)} custom-call(bf16[16,16,16,384]{3,2,1,0:T(8,128)(2,1)} %all-to-all-done.2.received, f32[8,256,768]{2,1,0:T(8,128)} %get-tuple-element.12.slope, bf16[2,256,256]{2,1,0:T(8,128)(2,1)} %constant.45.clone.col, bf16[2,384,48]{2,1,0:T(8,128)(2,1)} %bitcast.120, bf16[2,384,48]{2,1,0:T(8,128)(2,1)} %bitcast.122, ...), custom_call_target="tpu_custom_call" | custom-call | flops 8053063680 | bytes 12582912 | tf_op jit(solution)/shard_map/back/pallas_call | solution.py:277
  188.5 2.2 fusion.22
  190.7 0.1 dynamic-slice_bitcast_fusion.5
  190.9 1.7 collective-permute-start.12
  192.6 1.7 collective-permute-start.13
  194.2 2.0 collective-permute-start.14
  196.2 0.1 dynamic-slice_bitcast_fusion.2
  196.3 1.6 collective-permute-start.18
  197.9 0.5 collective-permute-start.19
  198.4 4.6 %collective-permute-done.12 = bf16[4,8,16,384]{3,2,1,0:T(8,128)(2,1)S(1)} collective-permute-done((bf16[4,8,16,384]{3,2,1,0:T(8,128)(2,1)S(1)}, bf16[4,8,16,384]{3,2,1,0:T(8,128)(2,1)S(1)}, u32[]{:S(2)}, u32[]{:S(2)}) %collective-permute-start.12) | collective-permute-done | bytes 393248 | tf_op jit(solution)/shard_map/ppermute | solution.py:342
  203.1 2.1 collective-permute-start.20
  205.2 5.5 %collective-permute-done.13 = bf16[4,8,16,384]{3,2,1,0:T(8,128)(2,1)S(1)} collective-permute-done((bf16[4,8,16,384]{3,2,1,0:T(8,128)(2,1)S(1)}, bf16[4,8,16,384]{3,2,1,0:T(8,128)(2,1)S(1)}, u32[]{:S(2)}, u32[]{:S(2)}) %collective-permute-start.13) | collective-permute-done | bytes 393248 | tf_op jit(solution)/shard_map/ppermute | solution.py:342
  210.6 1.8 collective-permute-done.14
  212.4 0.2 fusion.5
  212.7 1.6 collective-permute-start.15
  214.2 1.1 collective-permute-start.17
  215.3 2.2 collective-permute-start.16
  217.5 0.2 fusion.2
  217.8 1.2 collective-permute-start.21
  219.0 5.2 %collective-permute-start.23 = (bf16[8,16,384]{2,1,0:T(8,128)(2,1)S(1)}, bf16[8,16,384]{2,1,0:T(8,128)(2,1)S(1)}, u32[]{:S(2)}, u32[]{:S(2)}) collective-permute-start(bf16[8,16,384]{2,1,0:T(8,128)(2,1)S(1)} %get-tuple-element.34), channel_id=1, source_target_pairs={{0,32},{16,48},{32,0},{48,16},{64,96},{80,112},{96,64},{112,80},{1... | collective-permute-start | bytes 294920 | tf_op jit(solution)/shard_map/ppermute | solution.py:342
  224.2 2.5 collective-permute-start.22
  226.7 0.1 fusion.17
  226.8 0.9 collective-permute-done.23
  227.8 1.2 collective-permute-done.22
  229.0 0.1 fusion.14
  229.0 15.5 %all_to_all.25.spec = bf16[16,16,384]{2,1,0:T(8,128)(2,1)} all-to-all(bf16[16,16,384]{2,1,0:T(8,128)(2,1)S(1)} %pad_maximum_fusion.1), channel_id=1, replica_groups=mesh['dp'=16,'rows'=16] {'rows'}, dimensions={0} | all-to-all | bytes 393216 | tf_op jit(solution)/shard_map/all_to_all | solution.py:366
  244.6 1.9 grad_row.1
  246.4 14.1 %all_to_all.26 = bf16[16,16,384]{2,1,0:T(8,128)(2,1)} all-to-all(bf16[16,16,384]{2,1,0:T(8,128)(2,1)} %grad_row.1), channel_id=1, replica_groups=mesh['dp'=16,'rows'=16] {'dp'}, dimensions={0} | all-to-all | bytes 393216 | tf_op jit(solution)/shard_map/all_to_all | solution.py:366
  260.5 3.7 %all-to-all-start.1 = ((bf16[16,16,16,384]{3,2,1,0:T(8,128)(2,1)}), bf16[16,16,16,384]{3,2,1,0:T(8,128)(2,1)S(1)}, u32[]{:S(2)}, u32[]{:S(2)}) async-start(bf16[16,16,16,384]{3,2,1,0:T(8,128)(2,1)} %get-tuple-element.10), calls=%async_computation.1 | async-start | bytes 6291456 | tf_op jit(solution)/shard_map/all_to_all | solution.py:366
  264.3 1.7 convert_add_fusion.4
  266.0 70.0 %all-to-all-done.1.spec = bf16[16,16,16,384]{3,2,1,0:T(8,128)(2,1)S(1)} async-done(((bf16[16,16,16,384]{3,2,1,0:T(8,128)(2,1)}), bf16[16,16,16,384]{3,2,1,0:T(8,128)(2,1)S(1)}, u32[]{:S(2)}, u32[]{:S(2)}) %all-to-all-start.1) | async-done | bytes 3145760 | tf_op jit(solution)/shard_map/all_to_all | solution.py:366
  336.0 1.6 copy-done
  337.6 8.2 %finish.1 = bf16[16,256,384]{2,1,0:T(8,128)(2,1)} custom-call(bf16[256,256]{1,0:T(8,128)(2,1)} %constant.48.clone.table, bf16[16,16,16,384]{3,2,1,0:T(8,128)(2,1)} %copy-done, bf16[16,256,384]{2,1,0:T(8,128)(2,1)} %bitcast.114, bf16[16,256,384]{2,1,0:T(8,128)(2,1)} %prompt.3), custom_call_target="tpu_custom_call" | custom-call | flops 805306368 | bytes 12582912 | tf_op jit(solution)/shard_map/finish/pallas_call | solution.py:304
  (23 shorter events, 0.3 us)
Async XLA Ops:
  8.4 80.4 %all-to-all-start = ((bf16[16,16,16,384]{3,2,1,0:T(8,128)(2,1)}), bf16[16,16,16,384]{3,2,1,0:T(8,128)(2,1)S(1)}, u32[]{:S(2)}, u32[]{:S(2)}) async-start(bf16[16,16,16,384]{3,2,1,0:T(8,128)(2,1)} %rows_scene.1), calls=%async_computation | async-start | bytes 6291456 | tf_op jit(solution)/shard_map/all_to_all | solution.py:366
  88.8 1.7 copy-start.1
  90.5 76.5 %all-to-all-start.2 = ((bf16[16,16,16,384]{3,2,1,0:T(8,128)(2,1)}), bf16[16,16,16,384]{3,2,1,0:T(8,128)(2,1)}, u32[]{:S(2)}, u32[]{:S(2)}) async-start(bf16[16,16,16,384]{3,2,1,0:T(8,128)(2,1)} %get-tuple-element.11), calls=%async_computation.2 | async-start | bytes 6291456 | tf_op jit(solution)/shard_map/all_to_all | solution.py:366
  98.3 13.0 %collective-permute-start = (bf16[4,8,16,384]{3,2,1,0:T(8,128)(2,1)}, bf16[4,8,16,384]{3,2,1,0:T(8,128)(2,1)}, u32[]{:S(2)}, u32[]{:S(2)}) collective-permute-start(bf16[4,8,16,384]{3,2,1,0:T(8,128)(2,1)} %get-tuple-element.24), channel_id=1, source_target_pairs={{0,16},{16,32},{32,48},{48,0},{64,80},{80,96},{96,112},{112,64},{1... | collective-permute-start | bytes 1179656 | tf_op jit(solution)/shard_map/ppermute | solution.py:342
  99.9 13.5 %collective-permute-start.1 = (bf16[4,8,16,384]{3,2,1,0:T(8,128)(2,1)}, bf16[4,8,16,384]{3,2,1,0:T(8,128)(2,1)}, u32[]{:S(2)}, u32[]{:S(2)}) collective-permute-start(bf16[4,8,16,384]{3,2,1,0:T(8,128)(2,1)} %get-tuple-element.25), channel_id=1, source_target_pairs={{0,48},{16,0},{32,16},{48,32},{64,112},{80,64},{96,80},{112,96},{1... | collective-permute-start | bytes 1179656 | tf_op jit(solution)/shard_map/ppermute | solution.py:342
  101.6 19.3 %collective-permute-start.2 = (bf16[4,8,16,384]{3,2,1,0:T(8,128)(2,1)S(1)}, bf16[4,8,16,384]{3,2,1,0:T(8,128)(2,1)}, u32[]{:S(2)}, u32[]{:S(2)}) collective-permute-start(bf16[4,8,16,384]{3,2,1,0:T(8,128)(2,1)S(1)} %get-tuple-element.26), channel_id=1, source_target_pairs={{0,32},{16,48},{32,0},{48,16},{64,96},{80,112},{96,64},{112,80},{1... | collective-permute-start | bytes 1179656 | tf_op jit(solution)/shard_map/ppermute | solution.py:342
  103.7 21.4 %collective-permute-start.6 = (bf16[4,8,16,384]{3,2,1,0:T(8,128)(2,1)S(1)}, bf16[4,8,16,384]{3,2,1,0:T(8,128)(2,1)S(1)}, u32[]{:S(2)}, u32[]{:S(2)}) collective-permute-start(bf16[4,8,16,384]{3,2,1,0:T(8,128)(2,1)S(1)} %get-tuple-element.27), channel_id=1, source_target_pairs={{0,64},{16,80},{32,96},{48,112},{64,128},{80,144},{96,160},{112,17... | collective-permute-start | bytes 1179656 | tf_op jit(solution)/shard_map/ppermute | solution.py:342
  105.2 21.9 %collective-permute-start.7 = (bf16[4,8,16,384]{3,2,1,0:T(8,128)(2,1)S(1)}, bf16[4,8,16,384]{3,2,1,0:T(8,128)(2,1)S(1)}, u32[]{:S(2)}, u32[]{:S(2)}) collective-permute-start(bf16[4,8,16,384]{3,2,1,0:T(8,128)(2,1)S(1)} %get-tuple-element.28), channel_id=1, source_target_pairs={{0,192},{16,208},{32,224},{48,240},{64,0},{80,16},{96,32},{112,48}... | collective-permute-start | bytes 1179656 | tf_op jit(solution)/shard_map/ppermute | solution.py:342
  111.3 15.9 %collective-permute-start.8 = (bf16[4,8,16,384]{3,2,1,0:T(8,128)(2,1)S(1)}, bf16[4,8,16,384]{3,2,1,0:T(8,128)(2,1)S(1)}, u32[]{:S(2)}, u32[]{:S(2)}) collective-permute-start(bf16[4,8,16,384]{3,2,1,0:T(8,128)(2,1)S(1)} %get-tuple-element.29), channel_id=1, source_target_pairs={{0,128},{16,144},{32,160},{48,176},{64,192},{80,208},{96,224},{112... | collective-permute-start | bytes 1179656 | tf_op jit(solution)/shard_map/ppermute | solution.py:342
  122.4 11.1 %collective-permute-start.3 = (bf16[8,16,384]{2,1,0:T(8,128)(2,1)S(1)}, bf16[8,16,384]{2,1,0:T(8,128)(2,1)S(1)}, u32[]{:S(2)}, u32[]{:S(2)}) collective-permute-start(bf16[8,16,384]{2,1,0:T(8,128)(2,1)S(1)} %get-tuple-element.36), channel_id=1, source_target_pairs={{0,64},{16,80},{32,96},{48,112},{64,128},{80,144},{96,160},{112,17... | collective-permute-start | bytes 294920 | tf_op jit(solution)/shard_map/ppermute | solution.py:342
  123.9 12.1 %collective-permute-start.5 = (bf16[8,16,384]{2,1,0:T(8,128)(2,1)S(1)}, bf16[8,16,384]{2,1,0:T(8,128)(2,1)S(1)}, u32[]{:S(2)}, u32[]{:S(2)}) collective-permute-start(bf16[8,16,384]{2,1,0:T(8,128)(2,1)S(1)} %get-tuple-element.37), channel_id=1, source_target_pairs={{0,128},{16,144},{32,160},{48,176},{64,192},{80,208},{96,224},{112... | collective-permute-start | bytes 294920 | tf_op jit(solution)/shard_map/ppermute | solution.py:342
  125.0 11.0 %collective-permute-start.4 = (bf16[8,16,384]{2,1,0:T(8,128)(2,1)S(1)}, bf16[8,16,384]{2,1,0:T(8,128)(2,1)S(1)}, u32[]{:S(2)}, u32[]{:S(2)}) collective-permute-start(bf16[8,16,384]{2,1,0:T(8,128)(2,1)S(1)} %get-tuple-element.38), channel_id=1, source_target_pairs={{0,192},{16,208},{32,224},{48,240},{64,0},{80,16},{96,32},{112,48}... | collective-permute-start | bytes 294920 | tf_op jit(solution)/shard_map/ppermute | solution.py:342
  127.4 8.6 %collective-permute-start.9 = (bf16[8,16,384]{2,1,0:T(8,128)(2,1)S(1)}, bf16[8,16,384]{2,1,0:T(8,128)(2,1)S(1)}, u32[]{:S(2)}, u32[]{:S(2)}) collective-permute-start(bf16[8,16,384]{2,1,0:T(8,128)(2,1)S(1)} %get-tuple-element.39), channel_id=1, source_target_pairs={{0,16},{16,32},{32,48},{48,0},{64,80},{80,96},{96,112},{112,64},{1... | collective-permute-start | bytes 294920 | tf_op jit(solution)/shard_map/ppermute | solution.py:342
  128.7 8.4 %collective-permute-start.11 = (bf16[8,16,384]{2,1,0:T(8,128)(2,1)S(1)}, bf16[8,16,384]{2,1,0:T(8,128)(2,1)S(1)}, u32[]{:S(2)}, u32[]{:S(2)}) collective-permute-start(bf16[8,16,384]{2,1,0:T(8,128)(2,1)S(1)} %get-tuple-element.40), channel_id=1, source_target_pairs={{0,32},{16,48},{32,0},{48,16},{64,96},{80,112},{96,64},{112,80},{1... | collective-permute-start | bytes 294920 | tf_op jit(solution)/shard_map/ppermute | solution.py:342
  133.5 4.7 %collective-permute-start.10 = (bf16[8,16,384]{2,1,0:T(8,128)(2,1)S(1)}, bf16[8,16,384]{2,1,0:T(8,128)(2,1)S(1)}, u32[]{:S(2)}, u32[]{:S(2)}) collective-permute-start(bf16[8,16,384]{2,1,0:T(8,128)(2,1)S(1)} %get-tuple-element.41), channel_id=1, source_target_pairs={{0,48},{16,0},{32,16},{48,32},{64,112},{80,64},{96,80},{112,96},{1... | collective-permute-start | bytes 294920 | tf_op jit(solution)/shard_map/ppermute | solution.py:342
  190.9 12.2 %collective-permute-start.12 = (bf16[4,8,16,384]{3,2,1,0:T(8,128)(2,1)S(1)}, bf16[4,8,16,384]{3,2,1,0:T(8,128)(2,1)S(1)}, u32[]{:S(2)}, u32[]{:S(2)}) collective-permute-start(bf16[4,8,16,384]{3,2,1,0:T(8,128)(2,1)S(1)} %get-tuple-element.18), channel_id=1, source_target_pairs={{0,16},{16,32},{32,48},{48,0},{64,80},{80,96},{96,112},{112,64},{1... | collective-permute-start | bytes 1179656 | tf_op jit(solution)/shard_map/ppermute | solution.py:342
  192.6 18.1 %collective-permute-start.13 = (bf16[4,8,16,384]{3,2,1,0:T(8,128)(2,1)S(1)}, bf16[4,8,16,384]{3,2,1,0:T(8,128)(2,1)S(1)}, u32[]{:S(2)}, u32[]{:S(2)}) collective-permute-start(bf16[4,8,16,384]{3,2,1,0:T(8,128)(2,1)S(1)} %get-tuple-element.19), channel_id=1, source_target_pairs={{0,48},{16,0},{32,16},{48,32},{64,112},{80,64},{96,80},{112,96},{1... | collective-permute-start | bytes 1179656 | tf_op jit(solution)/shard_map/ppermute | solution.py:342
  194.2 18.2 %collective-permute-start.14 = (bf16[4,8,16,384]{3,2,1,0:T(8,128)(2,1)S(1)}, bf16[4,8,16,384]{3,2,1,0:T(8,128)(2,1)S(1)}, u32[]{:S(2)}, u32[]{:S(2)}) collective-permute-start(bf16[4,8,16,384]{3,2,1,0:T(8,128)(2,1)S(1)} %get-tuple-element.20), channel_id=1, source_target_pairs={{0,32},{16,48},{32,0},{48,16},{64,96},{80,112},{96,64},{112,80},{1... | collective-permute-start | bytes 1179656 | tf_op jit(solution)/shard_map/ppermute | solution.py:342
  196.3 19.0 %collective-permute-start.18 = (bf16[4,8,16,384]{3,2,1,0:T(8,128)(2,1)S(1)}, bf16[4,8,16,384]{3,2,1,0:T(8,128)(2,1)S(1)}, u32[]{:S(2)}, u32[]{:S(2)}) collective-permute-start(bf16[4,8,16,384]{3,2,1,0:T(8,128)(2,1)S(1)} %get-tuple-element.21), channel_id=1, source_target_pairs={{0,64},{16,80},{32,96},{48,112},{64,128},{80,144},{96,160},{112,17... | collective-permute-start | bytes 1179656 | tf_op jit(solution)/shard_map/ppermute | solution.py:342
  197.9 19.6 %collective-permute-start.19 = (bf16[4,8,16,384]{3,2,1,0:T(8,128)(2,1)S(1)}, bf16[4,8,16,384]{3,2,1,0:T(8,128)(2,1)S(1)}, u32[]{:S(2)}, u32[]{:S(2)}) collective-permute-start(bf16[4,8,16,384]{3,2,1,0:T(8,128)(2,1)S(1)} %get-tuple-element.22), channel_id=1, source_target_pairs={{0,192},{16,208},{32,224},{48,240},{64,0},{80,16},{96,32},{112,48}... | collective-permute-start | bytes 1179656 | tf_op jit(solution)/shard_map/ppermute | solution.py:342
  203.1 14.4 %collective-permute-start.20 = (bf16[4,8,16,384]{3,2,1,0:T(8,128)(2,1)S(1)}, bf16[4,8,16,384]{3,2,1,0:T(8,128)(2,1)S(1)}, u32[]{:S(2)}, u32[]{:S(2)}) collective-permute-start(bf16[4,8,16,384]{3,2,1,0:T(8,128)(2,1)S(1)} %get-tuple-element.23), channel_id=1, source_target_pairs={{0,128},{16,144},{32,160},{48,176},{64,192},{80,208},{96,224},{112... | collective-permute-start | bytes 1179656 | tf_op jit(solution)/shard_map/ppermute | solution.py:342
  212.7 11.5 %collective-permute-start.15 = (bf16[8,16,384]{2,1,0:T(8,128)(2,1)S(1)}, bf16[8,16,384]{2,1,0:T(8,128)(2,1)S(1)}, u32[]{:S(2)}, u32[]{:S(2)}) collective-permute-start(bf16[8,16,384]{2,1,0:T(8,128)(2,1)S(1)} %get-tuple-element.30), channel_id=1, source_target_pairs={{0,64},{16,80},{32,96},{48,112},{64,128},{80,144},{96,160},{112,17... | collective-permute-start | bytes 294920 | tf_op jit(solution)/shard_map/ppermute | solution.py:342
  214.2 12.5 %collective-permute-start.17 = (bf16[8,16,384]{2,1,0:T(8,128)(2,1)S(1)}, bf16[8,16,384]{2,1,0:T(8,128)(2,1)S(1)}, u32[]{:S(2)}, u32[]{:S(2)}) collective-permute-start(bf16[8,16,384]{2,1,0:T(8,128)(2,1)S(1)} %get-tuple-element.31), channel_id=1, source_target_pairs={{0,128},{16,144},{32,160},{48,176},{64,192},{80,208},{96,224},{112... | collective-permute-start | bytes 294920 | tf_op jit(solution)/shard_map/ppermute | solution.py:342
  215.3 11.4 %collective-permute-start.16 = (bf16[8,16,384]{2,1,0:T(8,128)(2,1)S(1)}, bf16[8,16,384]{2,1,0:T(8,128)(2,1)S(1)}, u32[]{:S(2)}, u32[]{:S(2)}) collective-permute-start(bf16[8,16,384]{2,1,0:T(8,128)(2,1)S(1)} %get-tuple-element.32), channel_id=1, source_target_pairs={{0,192},{16,208},{32,224},{48,240},{64,0},{80,16},{96,32},{112,48}... | collective-permute-start | bytes 294920 | tf_op jit(solution)/shard_map/ppermute | solution.py:342
  217.8 9.0 %collective-permute-start.21 = (bf16[8,16,384]{2,1,0:T(8,128)(2,1)S(1)}, bf16[8,16,384]{2,1,0:T(8,128)(2,1)S(1)}, u32[]{:S(2)}, u32[]{:S(2)}) collective-permute-start(bf16[8,16,384]{2,1,0:T(8,128)(2,1)S(1)} %get-tuple-element.33), channel_id=1, source_target_pairs={{0,16},{16,32},{32,48},{48,0},{64,80},{80,96},{96,112},{112,64},{1... | collective-permute-start | bytes 294920 | tf_op jit(solution)/shard_map/ppermute | solution.py:342
  219.0 8.8 %collective-permute-start.23 = (bf16[8,16,384]{2,1,0:T(8,128)(2,1)S(1)}, bf16[8,16,384]{2,1,0:T(8,128)(2,1)S(1)}, u32[]{:S(2)}, u32[]{:S(2)}) collective-permute-start(bf16[8,16,384]{2,1,0:T(8,128)(2,1)S(1)} %get-tuple-element.34), channel_id=1, source_target_pairs={{0,32},{16,48},{32,0},{48,16},{64,96},{80,112},{96,64},{112,80},{1... | collective-permute-start | bytes 294920 | tf_op jit(solution)/shard_map/ppermute | solution.py:342
  224.2 4.7 %collective-permute-start.22 = (bf16[8,16,384]{2,1,0:T(8,128)(2,1)S(1)}, bf16[8,16,384]{2,1,0:T(8,128)(2,1)S(1)}, u32[]{:S(2)}, u32[]{:S(2)}) collective-permute-start(bf16[8,16,384]{2,1,0:T(8,128)(2,1)S(1)} %get-tuple-element.35), channel_id=1, source_target_pairs={{0,48},{16,0},{32,16},{48,32},{64,112},{80,64},{96,80},{112,96},{1... | collective-permute-start | bytes 294920 | tf_op jit(solution)/shard_map/ppermute | solution.py:342
  260.5 75.5 %all-to-all-start.1 = ((bf16[16,16,16,384]{3,2,1,0:T(8,128)(2,1)}), bf16[16,16,16,384]{3,2,1,0:T(8,128)(2,1)S(1)}, u32[]{:S(2)}, u32[]{:S(2)}) async-start(bf16[16,16,16,384]{3,2,1,0:T(8,128)(2,1)} %get-tuple-element.10), calls=%async_computation.1 | async-start | bytes 6291456 | tf_op jit(solution)/shard_map/all_to_all | solution.py:366
  336.0 1.6 copy-start

commit v2 on v1

--- a/solution.py
+++ b/solution.py
@@ -58,27 +58,67 @@
     return pl.BlockSpec(shape, lambda i: (0,) * len(shape))
 
 
-HB = 2
+HB = 4
+FINISH_A = 2
+PAIRS = [(i, i + 1) for i in range(0, HB, 2)]
+
+
+def beside(left, right):
+    return jnp.concatenate([left, right], axis=1)
+
+
+def summed_row(scene, prompt, i):
+    return (scene[i].astype(F32) + prompt[i].astype(F32)).astype(BF)
+
+
+def put_rows(out, pair, value):
+    value = value.astype(BF)
+    for i, part in zip(pair, (value[:, :C], value[:, C:])):
+        out[:, i] = part.reshape(N, 16, C)
 
 
 def rows_scene_kernel(table, scene, prompt, out):
-    for i in range(HB):
-        summed = (scene[i].astype(F32) + prompt[i].astype(F32)).astype(BF)
-        out[:, i] = dot(table[...], summed).astype(BF).reshape(N, 16, C)
-
-
-def rows_cot_kernel(table, cot, out, pieces):
-    for i in range(HB):
-        x = cot[i]
-        out[:, i] = dot(table[...], x).astype(BF).reshape(N, 16, C)
-        pieces[:, i] = x.reshape(N, 16, C)
+    for i, j in PAIRS:
+        summed = beside(summed_row(scene, prompt, i), summed_row(scene, prompt, j))
+        put_rows(out, (i, j), dot(table[...], summed))
+
+
+def rows_cot_kernel(me, here, table, cot, *rest):
+    outs, pieces, ordered = rest[:N], rest[N : N + 4], rest[N + 4]
+
+    @pl.when(pl.program_id(0) == 0)
+    def _():
+        for j in range(N):
+            owner = (here[0] + j) & (N - 1)
+            ordered[j * 16 : (j + 1) * 16] = table[pl.ds(pl.multiple_of(owner * 16, 16), 16), :]
+
+    for i, j in PAIRS:
+        value = dot(ordered[...], beside(cot[i], cot[j])).astype(BF)
+        for step in range(N):
+            part = value[step * 16 : (step + 1) * 16]
+            outs[step][i] = part[:, :C]
+            outs[step][j] = part[:, C:]
+
+    x, y = me[0] >> 2, me[0] & 3
+
+    def slot(b, carry):
+        for a in range(4):
+            owner = ((x + b) & 3) * 4 + ((y + a) & 3)
+            rows = pl.ds(pl.multiple_of(owner * 16, 16), 16)
+            for i in range(HB):
+                pieces[a][b, i] = cot[i, rows, :]
+        return carry
+
+    lax.fori_loop(0, 4, slot, 0)
 
 
 GRID_SPEC = pl.BlockSpec((HB, W, C), lambda i: (i, 0, 0))
 SPEC_SPEC = pl.BlockSpec((N, HB, 16, C), lambda i: (0, i, 0, 0))
 SPEC_SHAPE = jax.ShapeDtypeStruct((N, N, 16, C), BF)
+PIECE_SHAPE = jax.ShapeDtypeStruct((4, N // 2, 16, C), BF)
 ROW_FLOPS = 2 * 256 * 256 * N * C
 ARRAY_BYTES = 2 * N * W * C
+ME_SPEC = pl.BlockSpec(memory_space=pltpu.SMEM)
 
 
 def rows_scene(scene, prompt):
@@ -93,16 +133,18 @@
     )(ROW_FWD, scene, prompt)
 
 
-def rows_cot(cot):
+def rows_cot(me, here, cot):
     return pl.pallas_call(
         rows_cot_kernel,
         grid=(N // HB,),
-        in_specs=[full((W, W)), GRID_SPEC],
-        out_specs=[SPEC_SPEC, SPEC_SPEC],
-        out_shape=[SPEC_SHAPE, SPEC_SHAPE],
+        in_specs=[ME_SPEC, ME_SPEC, full((W, W)), GRID_SPEC],
+        out_specs=[pl.BlockSpec((HB, 16, C), lambda i: (i, 0, 0))] * N
+        + [pl.BlockSpec((4, HB, 16, C), lambda i: (0, i, 0, 0))] * 4,
+        out_shape=[jax.ShapeDtypeStruct((N, 16, C), BF)] * N + [jax.ShapeDtypeStruct((4, N, 16, C), BF)] * 4,
+        scratch_shapes=[pltpu.VMEM((W, W), BF)],
         cost_estimate=cost(ROW_FLOPS, 3 * ARRAY_BYTES),
         name="rows_cot",
-    )(ROW_INV, cot)
+    )(me, here, ROW_INV, cot)
 
 
 LANES = 128
@@ -127,24 +169,25 @@
 def columns_of(wide, k):
     halves = []
     for q in range(2):
-        rows = pl.ds(q * K8 + k, H, stride=16)
-        halves.append(jnp.concatenate([wide[t, rows, :].astype(BF) for t in range(TILES)], axis=1))
+        parts = []
+        for kk in range(2):
+            rows = pl.ds(q * K8 + k + kk, H, stride=16)
+            parts += [wide[t, rows, :].astype(BF) for t in range(TILES)]
+        halves.append(jnp.concatenate(parts, axis=1))
     return jnp.concatenate(halves, axis=0)
 
 
 def store_columns(wide, k, value):
     for q in range(2):
-        rows = pl.ds(q * K8 + k, H, stride=16)
-        for t in range(TILES):
-            wide[t, rows, :] = value[q * H : (q + 1) * H, t * LANES : (t + 1) * LANES]
-
-
-def to_lanes(rows):
-    return jnp.concatenate([rows[:H], rows[H:]], axis=1)
-
-
-def to_rows(lanes):
-    return jnp.concatenate([lanes[:, :C], lanes[:, C:]], axis=0)
+        for kk in range(2):
+            rows = pl.ds(q * K8 + k + kk, H, stride=16)
+            for t in range(TILES):
+                lane = kk * C + t * LANES
+                wide[t, rows, :] = value[q * H : (q + 1) * H, lane : lane + LANES]
+
+
+def swap_pairs(value):
+    return jnp.concatenate([beside(value[:H, :C], value[H:, :C]), beside(value[:H, C:], value[H:, C:])], axis=0)
 
 
 def same_block(member):
@@ -177,7 +220,7 @@
 
 
 def mix_kernel(received, col, w1, b1, w2, b2, tile, member, out, slope, wide, dense1, dense2, col_fwd, col_inv):
-    k = pl.program_id(0)
+    k = pl.program_id(0) * 2
 
     @pl.when(k == 0)
     def _():
@@ -189,14 +232,14 @@
     spectrum = dot(col_fwd[...], columns_of(wide, k)).astype(BF)
     bias1 = jnp.concatenate([b1[0:1], b1[1:2]], axis=1)
     bias2 = jnp.concatenate([b2[0:1], b2[1:2]], axis=1)
-    z = dot(to_lanes(spectrum), dense1[...]) + bias1
+    z = dot(swap_pairs(spectrum), dense1[...]) + bias1
     cumulative = 0.5 * (1.0 + lax.erf(z * 0.7071067811865476))
     hidden = (z * cumulative).astype(BF)
-    slope[0] = cumulative + z * (jnp.exp(-0.5 * z * z) * 0.3989422804014327)
+    slope[...] = (cumulative + z * (jnp.exp(-0.5 * z * z) * 0.3989422804014327)).reshape(2, H, 2 * C)
     output = (dot(hidden, dense2[...]) + bias2).astype(BF)
-    store_columns(wide, k, dot(col_inv[...], to_rows(output)))
-
-    @pl.when(k == K8 - 1)
+    store_columns(wide, k, dot(col_inv[...], swap_pairs(output)))
+
+    @pl.when(k == K8 - 2)
     def _():
         def step(r, carry):
             out[r] = block_of(wide, r)
@@ -205,28 +248,51 @@
         lax.fori_loop(0, N, step, 0)
 
 
-def back_kernel(received, slope, col, w1, w2, tile, member, out, wide, dense1, dense2, col_fwd, col_inv):
-    k = pl.program_id(0)
+def back_kernel(me, here, *refs):
+    received, (slope, col, w1, w2, tile, member), rest = refs[:N], refs[N : N + 6], refs[N + 6 :]
+    pieces, (wide, dense1, dense2, col_fwd, col_inv, landed, arrived) = rest[:8], rest[8:]
+    k = pl.program_id(0) * 2
 
     @pl.when(k == 0)
     def _():
-        load_block(received, wide)
+        for j in range(N):
+            pltpu.make_async_copy(received[j], landed.at[j], arrived.at[j]).start()
         column_matrices(col, col_fwd, col_inv)
         expand_transposed(w1, tile, member, dense1)
         expand_transposed(w2, tile, member, dense2)
+        for j in range(N):
+            pltpu.make_async_copy(received[j], landed.at[j], arrived.at[j]).wait()
+
+        def step(j, carry):
+            source = (here[0] - j) & (N - 1)
+            rows = landed[j].astype(F32).reshape(256, C)
+            for t in range(TILES):
+                wide[t, pl.ds(pl.multiple_of(source * 256, 256), 256), :] = rows[:, t * LANES : (t + 1) * LANES]
+            return carry
+
+        lax.fori_loop(0, N, step, 0)
 
     back_out = dot(col_fwd[...], columns_of(wide, k)).astype(BF)
-    back_pre = (dot(to_lanes(back_out), dense2[...]) * slope[0]).astype(BF)
+    back_pre = (dot(swap_pairs(back_out), dense2[...]) * slope[...].reshape(2 * H, 2 * C)).astype(BF)
     back_spectrum = dot(back_pre, dense1[...]).astype(BF)
-    store_columns(wide, k, dot(col_inv[...], to_rows(back_spectrum)))
-
-    @pl.when(k == K8 - 1)
+    store_columns(wide, k, dot(col_inv[...], swap_pairs(back_spectrum)))
+
+    @pl.when(k == K8 - 2)
     def _():
-        def step(r, carry):
-            out[:, r] = block_of(wide, r)
-            return carry
-
-        lax.fori_loop(0, N, step, 0)
+        x, y = me[0] >> 2, me[0] & 3
+        for half in range(2):
+            for a in range(4):
+                for b in range(4):
+                    jx, jy = (b, a) if half == 0 else (a, b)
+                    owner = ((x + jx) & 3) * 4 + ((y + jy) & 3)
+
+                    def step(r, carry, a=a, b=b, half=half, owner=owner):
+                        rows = pl.ds(pl.multiple_of(((half * 8 + r) * 16 + owner) * 16, 16), 16)
+                        block = jnp.concatenate([wide[t, rows, :].astype(BF) for t in range(TILES)], axis=1)
+                        pieces[half * 4 + a][b, r] = block
+                        return carry
+
+                    lax.fori_loop(0, N // 2, step, 0)
 
 
 def column_matrices(col, col_fwd, col_inv):
@@ -246,7 +312,7 @@
     pltpu.VMEM((2 * H, 2 * H), BF),
     pltpu.VMEM((2 * H, 2 * H), BF),
 ]
-SLOPE_SPEC = pl.BlockSpec((1, H, 2 * C), lambda i: (i, 0, 0))
+SLOPE_SPEC = pl.BlockSpec((2, H, 2 * C), lambda i: (i, 0, 0))
 SLOPE_SHAPE = jax.ShapeDtypeStruct((K8, H, 2 * C), F32)
 FULL_SPEC = full((N, N, 16, C))
 
@@ -254,7 +320,7 @@
 def mix(received, w1, b1, w2, b2):
     return pl.pallas_call(
         mix_kernel,
-        grid=(K8,),
+        grid=(K8 // 2,),
         in_specs=[
             FULL_SPEC,
             full((2, H, H)),
@@ -273,12 +339,14 @@
     )(received, COL, w1, b1, w2, b2, TILE, BLOCK_OF)
 
 
-def back(received, slope, w1, w2):
+def back(me, here, received, slope, w1, w2):
     return pl.pallas_call(
         back_kernel,
-        grid=(K8,),
+        grid=(K8 // 2,),
         in_specs=[
-            FULL_SPEC,
+            ME_SPEC,
+            ME_SPEC,
+            *[pl.BlockSpec(memory_space=pl.ANY)] * N,
             SLOPE_SPEC,
             full((2, H, H)),
             full((2, C, BS)),
@@ -286,34 +354,44 @@
             full((BS, C)),
             full((C, NB)),
         ],
-        out_specs=FULL_SPEC,
-        out_shape=SPEC_SHAPE,
-        scratch_shapes=MIX_SCRATCH,
+        out_specs=[full(PIECE_SHAPE.shape)] * 8,
+        out_shape=[PIECE_SHAPE] * 8,
+        scratch_shapes=MIX_SCRATCH + [pltpu.VMEM((N, N, 16, C), BF), pltpu.SemaphoreType.DMA((N,))],
         cost_estimate=cost(MIX_FLOPS, 4 * ARRAY_BYTES),
         name="back",
-    )(received, slope, COL, w1, w2, TILE, BLOCK_OF)
-
-
-def finish_kernel(table, spec, scene, prompt, out):
-    for i in range(HB):
-        summed = (scene[i].astype(F32) + prompt[i].astype(F32)).astype(BF).astype(F32)
-        out[i] = (summed + dot(table[...], spec[:, i].reshape(W, C))).astype(BF)
-
-
-def finish(spec, scene, prompt):
+    )(me, here, *received, slope, COL, w1, w2, TILE, BLOCK_OF)
+
+
+def transposed_dot(table, value):
+    return lax.dot_general(table, value, (((0,), (0,)), ((), ())), preferred_element_type=F32)
+
+
+def finish_kernel(table, spec, scene, prompt, *rest):
+    out = rest[-1]
+    for i, j in PAIRS:
+        value = transposed_dot(table[...], beside(spec[:, i].reshape(W, C), spec[:, j].reshape(W, C)))
+        for row, part in ((i, value[:, :C]), (j, value[:, C:])):
+            out[row] = (summed_row(scene, prompt, row).astype(F32) + part).astype(BF)
+
+
+def finish(spec, scene, prompt, first, steps, into=None):
+    grid_spec = pl.BlockSpec((HB, W, C), lambda i: (i + first, 0, 0))
+    spec_spec = pl.BlockSpec((N, HB, 16, C), lambda i: (0, i + first, 0, 0))
+    more = [] if into is None else [into]
     return pl.pallas_call(
         finish_kernel,
-        grid=(N // HB,),
-        in_specs=[full((W, W)), SPEC_SPEC, GRID_SPEC, GRID_SPEC],
-        out_specs=GRID_SPEC,
+        grid=(steps,),
+        in_specs=[full((W, W)), spec_spec, grid_spec, grid_spec] + [pl.BlockSpec(memory_space=pl.ANY)] * len(more),
+        out_specs=grid_spec,
         out_shape=jax.ShapeDtypeStruct((N, W, C), BF),
-        cost_estimate=cost(ROW_FLOPS, 4 * ARRAY_BYTES),
-        name="finish",
-    )(np.ascontiguousarray(ROW_INV.T), spec, scene, prompt)
+        input_output_aliases={4: 0} if more else {},
+        cost_estimate=cost(ROW_FLOPS * steps * HB // N, 4 * ARRAY_BYTES * steps * HB // N),
+        name="finish_b" if more else "finish_a",
+    )(ROW_INV, spec, scene, prompt, *more)
 
 
 def grad_row_kernel(table, spec, out):
-    out[...] = dot(table[...], spec[...].reshape(W, C)).astype(BF).reshape(N, 16, C)
+    out[...] = transposed_dot(table[...], spec[...].reshape(W, C)).astype(BF).reshape(N, 16, C)
 
 
 def grad_row(spec):
@@ -325,22 +403,7 @@
         out_shape=jax.ShapeDtypeStruct((N, 16, C), BF),
         cost_estimate=cost(ROW_FLOPS // N, 2 * ARRAY_BYTES // N),
         name="grad_row",
-    )(np.ascontiguousarray(ROW_FWD.T), spec)
-
-
-def shifted_sum(parts, axis, mine, perm_of):
-    def piece_for(index):
-        starts = [jnp.uint32(0)] * parts.ndim
-        starts[axis] = index
-        sizes = list(parts.shape)
-        sizes[axis] = 1
-        return lax.squeeze(lax.dynamic_slice(parts, starts, sizes), (axis,))
-
-    total = piece_for(mine).astype(F32)
-    for j in (1, 3, 2):
-        piece = piece_for((mine + j) & 3)
-        total = total + lax.ppermute(piece, "dp", perm_of(j)).astype(F32)
-    return total
+    )(ROW_FWD, spec)
 
 
 def along_x(j):
@@ -351,15 +414,35 @@
     return [(x * 4 + y, x * 4 + (y + j) % 4) for x in range(4) for y in range(4)]
 
 
+def shifted_sum(pieces, perm_of):
+    received = [lax.ppermute(pieces[j], "dp", perm_of(j)) for j in (1, 3, 2)]
+    total = pieces[0].astype(F32)
+    for piece in received:
+        total = total + piece.astype(F32)
+    return total
+
+
 def sum_over_dp(pieces):
-    me = lax.axis_index("dp").astype(jnp.uint32)
-    x, y = me >> 2, me & 3
-    split = pieces.reshape(4, 4, 2, N // 2, 16, C)
-    first = shifted_sum(split[:, :, 0], 1, y, along_y).astype(BF)
-    second = shifted_sum(split[:, :, 1], 0, x, along_x).astype(BF)
-    first = shifted_sum(first, 0, x, along_x)
-    second = shifted_sum(second, 0, y, along_y)
+    first = shifted_sum(pieces[:4], along_y).astype(BF)
+    second = shifted_sum(pieces[4:], along_x).astype(BF)
+    first = shifted_sum([first[j] for j in range(4)], along_x)
+    second = shifted_sum([second[j] for j in range(4)], along_y)
     return jnp.concatenate([first, second], axis=0)
+
+
+def plain_sum_over_dp(pieces):
+    along = shifted_sum(pieces, along_y).astype(BF)
+    return shifted_sum([along[i] for i in range(4)], along_x)
+
+
+SEND_ORDER = (8, 7, 9, 6, 10, 5, 11, 4, 12, 3, 13, 2, 14, 1, 15)
+
+
+def send_round(pieces):
+    received = {0: pieces[0]}
+    for j in SEND_ORDER:
+        received[j] = lax.ppermute(pieces[j], "rows", [(i, (i + j) % N) for i in range(N)])
+    return [received[j] for j in range(N)]
 
 
 def exchange(blocks, axis):
@@ -370,16 +453,20 @@
     scene, cot = scenes[0], cotangent[0]
     w1 = first_weight.reshape(2, C, BS)
     w2 = second_weight.reshape(2, C, BS)
+    here = lax.axis_index("rows").reshape(1)
+    me = lax.axis_index("dp").reshape(1)
     scene_cols = exchange(rows_scene(scene, prompt), "rows")
-    cot_rows, cot_pieces = rows_cot(cot)
-    cot_cols = exchange(cot_rows, "rows")
-    cot_sum = sum_over_dp(cot_pieces)
+    leaving = rows_cot(me, here, cot)
+    cot_sum = plain_sum_over_dp(leaving[N:])
+    cot_cols = send_round(leaving[:N])
     scene_cols, cot_sum = lax.optimization_barrier((scene_cols, cot_sum))
     mixed_cols, slope = mix(scene_cols, w1, first_bias, w2, second_bias)
     mixed_rows = exchange(mixed_cols, "rows")
-    grad_sum = sum_over_dp(back(cot_cols, slope, w1, w2)).astype(BF)
-    mixed = finish(mixed_rows, scene, prompt)
-    grad_rows = exchange(grad_row(exchange(grad_sum, "rows")), "dp")
+    grad_sum = sum_over_dp(back(me, here, cot_cols, slope, w1, w2)).astype(BF)
+    grad_cols = exchange(grad_sum, "rows")
+    mixed = finish(mixed_rows, scene, prompt, 0, FINISH_A)
+    grad_rows = exchange(grad_row(grad_cols), "dp")
+    mixed = finish(mixed_rows, scene, prompt, FINISH_A, N // HB - FINISH_A, mixed)
     prompt_grad = grad_rows.astype(F32) + cot_sum
     return (mixed[None], prompt_grad)
 

time: 349 us -> 374 us (1.072)
  waiting for transfers between devices: 169 us -> 198 us
  starting transfers between devices: 63.1 us -> 78.7 us
  Pallas kernels: 69.7 us -> 59.5 us
  local copies, waits for them, and re-layouts: 9.28 us -> 1.78 us
    ppermute x24 -> x33, waiting for transfers between devices: 29.2 us -> 127 us  [the longest x15 81.7 us: send_round(): lax.ppermute(pieces[j], 'rows', [(i, (i + j) % N) for i in range(N)])]
    all_to_all x3 -> x2, waiting for transfers between devices: 140 us -> 70 us  [exchange(): return lax.all_to_all(blocks, axis, split_axis=0, concat_axis=0, tiled=True)]
    ppermute x24 -> x33, starting transfers between devices: 46.1 us -> 66.4 us  [the longest x15 34 us: send_round(): lax.ppermute(pieces[j], 'rows', [(i, (i + j) % N) for i in range(N)])]
    pallas_call x4 -> x5, Pallas kernels: 60 us -> 51.9 us  [the longest x1 19.7 us: back(): pl.pallas_call(back_kernel, grid=(K8 // 2,), in_specs=[ME_SPEC, ME_SPEC,...]
    all_to_all x3 -> x2, starting transfers between devices: 17 us -> 12.3 us  [exchange(): return lax.all_to_all(blocks, axis, split_axis=0, concat_axis=0, tiled=True)]
    slice x2 -> x0, local copies, waits for them, and re-layouts: 4.41 us -> none  [sum_over_dp(): first = shifted_sum(split[:, :, 0], 1, y, along_y).astype(BF)]
  transfers between devices with their start and end apart: 27 -> 35, of which waited for: 12 -> 18; matrix products, arithmetic and copies ran while one was open for 2% -> 2% of each run, Pallas kernels for 9% -> 7%
where the time goes in v2:
time: 374 us; the launch traced here: 372 us
  waiting for transfers between devices  198 us (53%)
  starting transfers between devices  78.7 us (21%)
  Pallas kernels  59.5 us (16%)
  blocking collectives  27.9 us (7%)
  other arithmetic  5.89 us (2%)
    ppermute x15, waiting for transfers between devices, send_round(): lax.ppermute(pieces[j], 'rows', [(i, (i + j) % N) for i in range(N)])  81.7 us
    all_to_all x2, waiting for transfers between devices, exchange(): return lax.all_to_all(blocks, axis, split_axis=0, concat_axis=0, tiled=True)  70 us
    ppermute x18, waiting for transfers between devices, shifted_sum(): received = [lax.ppermute(pieces[j], 'dp', perm_of(j)) for j in (1, 3, 2)]  45.8 us
    ppermute x15, starting transfers between devices, send_round(): lax.ppermute(pieces[j], 'rows', [(i, (i + j) % N) for i in range(N)])  34 us
    ppermute x18, starting transfers between devices, shifted_sum(): received = [lax.ppermute(pieces[j], 'dp', perm_of(j)) for j in (1, 3, 2)]  32.4 us
    all_to_all x2, blocking collectives, exchange(): return lax.all_to_all(blocks, axis, split_axis=0, concat_axis=0, tiled=True)  27.9 us
    pallas_call x1, Pallas kernels, back(): pl.pallas_call(back_kernel, grid=(K8 // 2,), in_specs=[ME_SPEC, ME_SPEC,...  19.7 us
    pallas_call x1, Pallas kernels, mix(): pl.pallas_call(mix_kernel, grid=(K8 // 2,), in_specs=[FULL_SPEC, full((2,...  18.9 us
  transfers between devices with their start and end apart: 35, of which 18 were waited for; matrix products, arithmetic and copies ran while one was open for 2% of the time, Pallas kernels for 7%

profile of v2, /device:TPU:2, one launch (start us, length us, event | category | flops | bytes accessed | tf_op | source)
XLA Modules:
  0.0 372.1 jit_solution(17559608811813535304)
XLA Ops:
  0.6 5.6 %rows_scene.1 = bf16[16,16,16,384]{3,2,1,0:T(8,128)(2,1)} custom-call(bf16[256,256]{1,0:T(8,128)(2,1)} %constant.17.clone.table, bf16[16,256,384]{2,1,0:T(8,128)(2,1)} %bitcast.40, bf16[16,256,384]{2,1,0:T(8,128)(2,1)} %prompt.5), custom_call_target="tpu_custom_call" | custom-call | flops 805306368 | bytes 9437184 | tf_op jit(solution)/shard_map/rows_scene/pallas_call | solution.py:125
  6.2 8.6 %all-to-all-start = ((bf16[16,16,16,384]{3,2,1,0:T(8,128)(2,1)}), bf16[16,16,16,384]{3,2,1,0:T(8,128)(2,1)S(1)}, u32[]{:S(2)}, u32[]{:S(2)}) async-start(bf16[16,16,16,384]{3,2,1,0:T(8,128)(2,1)} %rows_scene.1), calls=%async_computation | async-start | bytes 6291456 | tf_op jit(solution)/shard_map/all_to_all | solution.py:449
  14.8 5.8 %rows_cot.1 = (bf16[16,16,384]{2,1,0:T(8,128)(2,1)}, bf16[16,16,384]{2,1,0:T(8,128)(2,1)}, bf16[16,16,384]{2,1,0:T(8,128)(2,1)}, bf16[16,16,384]{2,1,0:T(8,128)(...) custom-call(s32[1]{0:T(128)} %bitcast.1.me, ...), custom_call_target="tpu_custom_call" | custom-call | flops 805306368 | bytes 9437184 | tf_op jit(solution)/shard_map/rows_cot/pallas_call | solution.py:137
  20.7 1.7 collective-permute-start
  22.3 1.7 collective-permute-start.1
  24.0 2.0 collective-permute-start.2
  26.0 1.9 collective-permute-start.7
  27.9 14.2 %collective-permute-done = bf16[4,16,16,384]{3,2,1,0:T(8,128)(2,1)S(1)} collective-permute-done((bf16[4,16,16,384]{3,2,1,0:T(8,128)(2,1)}, bf16[4,16,16,384]{3,2,1,0:T(8,128)(2,1)S(1)}, u32[]{:S(2)}, u32[]{:S(2)}) %collective-permute-start) | collective-permute-done | bytes 786464 | tf_op jit(solution)/shard_map/ppermute | solution.py:418
  42.0 0.6 collective-permute-start.8
  42.6 15.8 %collective-permute-done.1 = bf16[4,16,16,384]{3,2,1,0:T(8,128)(2,1)S(1)} collective-permute-done((bf16[4,16,16,384]{3,2,1,0:T(8,128)(2,1)}, bf16[4,16,16,384]{3,2,1,0:T(8,128)(2,1)S(1)}, u32[]{:S(2)}, u32[]{:S(2)}) %collective-permute-start.1) | collective-permute-done | bytes 786464 | tf_op jit(solution)/shard_map/ppermute | solution.py:418
  58.4 2.5 collective-permute-start.9
  60.9 0.6 collective-permute-start.10
  61.5 1.6 add_convert_fusion
  63.1 27.2 %collective-permute-done.6.refs_1_ = bf16[16,16,384]{2,1,0:T(8,128)(2,1)S(1)} collective-permute-done((bf16[16,16,384]{2,1,0:T(8,128)(2,1)}, bf16[16,16,384]{2,1,0:T(8,128)(2,1)S(1)}, u32[]{:S(2)}, u32[]{:S(2)}) %collective-permute-start.6) | collective-permute-done | bytes 196640 | tf_op jit(solution)/shard_map/ppermute | solution.py:444
  90.3 1.5 collective-permute-start.3
  91.8 1.8 collective-permute-start.5
  93.5 8.4 %collective-permute-done.8.refs_3_ = bf16[16,16,384]{2,1,0:T(8,128)(2,1)S(1)} collective-permute-done((bf16[16,16,384]{2,1,0:T(8,128)(2,1)}, bf16[16,16,384]{2,1,0:T(8,128)(2,1)S(1)}, u32[]{:S(2)}, u32[]{:S(2)}) %collective-permute-start.8) | collective-permute-done | bytes 196640 | tf_op jit(solution)/shard_map/ppermute | solution.py:444
  101.9 0.5 collective-permute-start.4
  102.4 1.4 collective-permute-done.9.refs_4_
  103.9 4.1 %collective-permute-start.11 = (bf16[16,16,384]{2,1,0:T(8,128)(2,1)}, bf16[16,16,384]{2,1,0:T(8,128)(2,1)}, u32[]{:S(2)}, u32[]{:S(2)}) collective-permute-start(bf16[16,16,384]{2,1,0:T(8,128)(2,1)} %get-tuple-element.46), channel_id=1, source_target_pairs={{0,6},{1,7},{2,8},{3,9},{4,10},{5,11},{6,12},{7,13},{8,14},{9,15},... | collective-permute-start | bytes 589832 | tf_op jit(solution)/shard_map/ppermute | solution.py:444
  107.9 17.9 %collective-permute-done.10.refs_5_ = bf16[16,16,384]{2,1,0:T(8,128)(2,1)S(1)} collective-permute-done((bf16[16,16,384]{2,1,0:T(8,128)(2,1)}, bf16[16,16,384]{2,1,0:T(8,128)(2,1)S(1)}, u32[]{:S(2)}, u32[]{:S(2)}) %collective-permute-start.10) | collective-permute-done | bytes 196640 | tf_op jit(solution)/shard_map/ppermute | solution.py:444
  125.8 0.1 collective-permute-start.13
  126.0 5.6 %collective-permute-start.14 = (bf16[16,16,384]{2,1,0:T(8,128)(2,1)}, bf16[16,16,384]{2,1,0:T(8,128)(2,1)}, u32[]{:S(2)}, u32[]{:S(2)}) collective-permute-start(bf16[16,16,384]{2,1,0:T(8,128)(2,1)} %get-tuple-element.49), channel_id=1, source_target_pairs={{0,9},{1,10},{2,11},{3,12},{4,13},{5,14},{6,15},{7,0},{8,1},{9,2},... | collective-permute-start | bytes 589832 | tf_op jit(solution)/shard_map/ppermute | solution.py:444
  131.6 1.6 collective-permute-start.15
  133.2 0.1 fusion.1
  133.4 5.3 %collective-permute-start.16 = (bf16[16,16,384]{2,1,0:T(8,128)(2,1)}, bf16[16,16,384]{2,1,0:T(8,128)(2,1)}, u32[]{:S(2)}, u32[]{:S(2)}) collective-permute-start(bf16[16,16,384]{2,1,0:T(8,128)(2,1)} %get-tuple-element.51), channel_id=1, source_target_pairs={{0,11},{1,12},{2,13},{3,14},{4,15},{5,0},{6,1},{7,2},{8,3},{9,4},{... | collective-permute-start | bytes 589832 | tf_op jit(solution)/shard_map/ppermute | solution.py:444
  138.7 5.6 %collective-permute-done.12.refs_7_ = bf16[16,16,384]{2,1,0:T(8,128)(2,1)} collective-permute-done((bf16[16,16,384]{2,1,0:T(8,128)(2,1)}, bf16[16,16,384]{2,1,0:T(8,128)(2,1)}, u32[]{:S(2)}, u32[]{:S(2)}) %collective-permute-start.12) | collective-permute-done | bytes 196640 | tf_op jit(solution)/shard_map/ppermute | solution.py:444
  144.3 8.0 %collective-permute-start.17 = (bf16[16,16,384]{2,1,0:T(8,128)(2,1)}, bf16[16,16,384]{2,1,0:T(8,128)(2,1)}, u32[]{:S(2)}, u32[]{:S(2)}) collective-permute-start(bf16[16,16,384]{2,1,0:T(8,128)(2,1)} %get-tuple-element.52), channel_id=1, source_target_pairs={{0,12},{1,13},{2,14},{3,15},{4,0},{5,1},{6,2},{7,3},{8,4},{9,5},{1... | collective-permute-start | bytes 589832 | tf_op jit(solution)/shard_map/ppermute | solution.py:444
  152.3 3.7 collective-permute-start.18
  156.0 7.3 %collective-permute-done.14.refs_9_ = bf16[16,16,384]{2,1,0:T(8,128)(2,1)} collective-permute-done((bf16[16,16,384]{2,1,0:T(8,128)(2,1)}, bf16[16,16,384]{2,1,0:T(8,128)(2,1)}, u32[]{:S(2)}, u32[]{:S(2)}) %collective-permute-start.14) | collective-permute-done | bytes 196640 | tf_op jit(solution)/shard_map/ppermute | solution.py:444
  163.3 3.4 collective-permute-done.15.refs_10_
  166.7 18.9 %mix.1 = (bf16[16,16,16,384]{3,2,1,0:T(8,128)(2,1)}, f32[8,256,768]{2,1,0:T(8,128)}) custom-call(bf16[16,16,16,384]{3,2,1,0:T(8,128)(2,1)} %copy-done.1, bf16[2,256,256]{2,1,0:T(8,128)(2,1)} %constant.19.clone.col.refs_17_, bf16[2,384,48]{2,1,0:T(8,128)(2,1)} %bitcast.45, f32[2,384]{1,0:T(2,128)} %b1.1, bf16[2,384,48]{2,1,0:T(8,128)(2,1)} %bitcast.47, ...), custom_call_target="tpu_custom_call" | custom-call | flops 8053063680 | bytes 12582912 | tf_op jit(solution)/shard_map/mix/pallas_call | solution.py:321
  185.6 7.3 %collective-permute-done.18.refs_13_ = bf16[16,16,384]{2,1,0:T(8,128)(2,1)} collective-permute-done((bf16[16,16,384]{2,1,0:T(8,128)(2,1)}, bf16[16,16,384]{2,1,0:T(8,128)(2,1)}, u32[]{:S(2)}, u32[]{:S(2)}) %collective-permute-start.18) | collective-permute-done | bytes 196640 | tf_op jit(solution)/shard_map/ppermute | solution.py:444
  192.9 0.3 collective-permute-done.19.refs_14_
  193.2 2.9 collective-permute-done.20.refs_15_
  196.2 19.7 %back.1 = (bf16[4,8,16,384]{3,2,1,0:T(8,128)(2,1)}, bf16[4,8,16,384]{3,2,1,0:T(8,128)(2,1)}, bf16[4,8,16,384]{3,2,1,0:T(8,128)(2,1)}, bf16[4,8,16,384]{3,2,1,0:T...) custom-call(s32[1]{0:T(128)} %bitcast.1.me, ...), custom_call_target="tpu_custom_call" | custom-call | flops 8053063680 | bytes 12582912 | tf_op jit(solution)/shard_map/back/pallas_call | solution.py:343
  215.9 1.6 collective-permute-start.21
  217.5 1.7 collective-permute-start.22
  219.2 2.0 collective-permute-start.23
  221.2 1.5 collective-permute-start.27
  222.7 0.5 collective-permute-start.28
  223.2 6.1 %collective-permute-done.21 = bf16[4,8,16,384]{3,2,1,0:T(8,128)(2,1)S(1)} collective-permute-done((bf16[4,8,16,384]{3,2,1,0:T(8,128)(2,1)}, bf16[4,8,16,384]{3,2,1,0:T(8,128)(2,1)S(1)}, u32[]{:S(2)}, u32[]{:S(2)}) %collective-permute-start.21) | collective-permute-done | bytes 393248 | tf_op jit(solution)/shard_map/ppermute | solution.py:418
  229.4 2.1 collective-permute-start.29
  231.5 5.8 %collective-permute-done.22 = bf16[4,8,16,384]{3,2,1,0:T(8,128)(2,1)S(1)} collective-permute-done((bf16[4,8,16,384]{3,2,1,0:T(8,128)(2,1)}, bf16[4,8,16,384]{3,2,1,0:T(8,128)(2,1)S(1)}, u32[]{:S(2)}, u32[]{:S(2)}) %collective-permute-start.22) | collective-permute-done | bytes 393248 | tf_op jit(solution)/shard_map/ppermute | solution.py:418
  237.3 1.7 collective-permute-done.23
  239.0 1.2 add_convert_fusion.2
  240.2 1.6 collective-permute-start.24
  241.8 1.1 collective-permute-start.26
  242.9 2.2 collective-permute-start.25
  245.1 1.2 add_convert_fusion.1
  246.3 1.2 collective-permute-start.30
  247.6 5.3 %collective-permute-start.32 = (bf16[8,16,384]{2,1,0:T(8,128)(2,1)S(1)}, bf16[8,16,384]{2,1,0:T(8,128)(2,1)S(1)}, u32[]{:S(2)}, u32[]{:S(2)}) collective-permute-start(bf16[8,16,384]{2,1,0:T(8,128)(2,1)S(1)} %get-tuple-element.73), channel_id=1, source_target_pairs={{0,32},{16,48},{32,0},{48,16},{64,96},{80,112},{96,64},{112,80},{1... | collective-permute-start | bytes 294920 | tf_op jit(solution)/shard_map/ppermute | solution.py:418
  252.8 2.5 collective-permute-start.31
  255.4 0.9 collective-permute-done.32
  256.4 1.2 collective-permute-done.31
  257.7 13.1 %all_to_all.20.spec = bf16[16,16,384]{2,1,0:T(8,128)(2,1)} all-to-all(bf16[16,16,384]{2,1,0:T(8,128)(2,1)S(1)} %pad_maximum_fusion), channel_id=1, replica_groups=mesh['dp'=16,'rows'=16] {'rows'}, dimensions={0} | all-to-all | bytes 393216 | tf_op jit(solution)/shard_map/all_to_all | solution.py:449
  270.7 1.9 grad_row.1
  272.7 14.9 %all_to_all.21 = bf16[16,16,384]{2,1,0:T(8,128)(2,1)} all-to-all(bf16[16,16,384]{2,1,0:T(8,128)(2,1)} %grad_row.1), channel_id=1, replica_groups=mesh['dp'=16,'rows'=16] {'dp'}, dimensions={0} | all-to-all | bytes 393216 | tf_op jit(solution)/shard_map/all_to_all | solution.py:449
  287.5 3.7 %all-to-all-start.1 = ((bf16[16,16,16,384]{3,2,1,0:T(8,128)(2,1)}), bf16[16,16,16,384]{3,2,1,0:T(8,128)(2,1)S(1)}, u32[]{:S(2)}, u32[]{:S(2)}) async-start(bf16[16,16,16,384]{3,2,1,0:T(8,128)(2,1)} %get-tuple-element.39), calls=%async_computation.1 | async-start | bytes 6291456 | tf_op jit(solution)/shard_map/all_to_all | solution.py:449
  291.3 1.7 convert_add_fusion.1
  293.0 70.0 %all-to-all-done.1.spec = bf16[16,16,16,384]{3,2,1,0:T(8,128)(2,1)S(1)} async-done(((bf16[16,16,16,384]{3,2,1,0:T(8,128)(2,1)}), bf16[16,16,16,384]{3,2,1,0:T(8,128)(2,1)S(1)}, u32[]{:S(2)}, u32[]{:S(2)}) %all-to-all-start.1) | async-done | bytes 3145760 | tf_op jit(solution)/shard_map/all_to_all | solution.py:449
  363.0 1.6 copy-done
  364.6 3.7 finish_a.1.rest_0_
  368.4 3.7 finish_b.1
  (40 shorter events, 0.3 us)
Async XLA Ops:
  6.2 127.1 %all-to-all-start = ((bf16[16,16,16,384]{3,2,1,0:T(8,128)(2,1)}), bf16[16,16,16,384]{3,2,1,0:T(8,128)(2,1)S(1)}, u32[]{:S(2)}, u32[]{:S(2)}) async-start(bf16[16,16,16,384]{3,2,1,0:T(8,128)(2,1)} %rows_scene.1), calls=%async_computation | async-start | bytes 6291456 | tf_op jit(solution)/shard_map/all_to_all | solution.py:449
  20.7 21.4 %collective-permute-start = (bf16[4,16,16,384]{3,2,1,0:T(8,128)(2,1)}, bf16[4,16,16,384]{3,2,1,0:T(8,128)(2,1)S(1)}, u32[]{:S(2)}, u32[]{:S(2)}) collective-permute-start(bf16[4,16,16,384]{3,2,1,0:T(8,128)(2,1)} %get-tuple-element.35), channel_id=1, source_target_pairs={{0,16},{16,32},{32,48},{48,0},{64,80},{80,96},{96,112},{112,64},{1... | collective-permute-start | bytes 2359304 | tf_op jit(solution)/shard_map/ppermute | solution.py:418
  22.3 36.1 %collective-permute-start.1 = (bf16[4,16,16,384]{3,2,1,0:T(8,128)(2,1)}, bf16[4,16,16,384]{3,2,1,0:T(8,128)(2,1)S(1)}, u32[]{:S(2)}, u32[]{:S(2)}) collective-permute-start(bf16[4,16,16,384]{3,2,1,0:T(8,128)(2,1)} %get-tuple-element.36), channel_id=1, source_target_pairs={{0,48},{16,0},{32,16},{48,32},{64,112},{80,64},{96,80},{112,96},{1... | collective-permute-start | bytes 2359304 | tf_op jit(solution)/shard_map/ppermute | solution.py:418
  24.0 36.9 %collective-permute-start.2 = (bf16[4,16,16,384]{3,2,1,0:T(8,128)(2,1)}, bf16[4,16,16,384]{3,2,1,0:T(8,128)(2,1)S(1)}, u32[]{:S(2)}, u32[]{:S(2)}) collective-permute-start(bf16[4,16,16,384]{3,2,1,0:T(8,128)(2,1)} %get-tuple-element.37), channel_id=1, source_target_pairs={{0,32},{16,48},{32,0},{48,16},{64,96},{80,112},{96,64},{112,80},{1... | collective-permute-start | bytes 2359304 | tf_op jit(solution)/shard_map/ppermute | solution.py:418
  26.0 64.3 %collective-permute-start.6 = (bf16[16,16,384]{2,1,0:T(8,128)(2,1)}, bf16[16,16,384]{2,1,0:T(8,128)(2,1)S(1)}, u32[]{:S(2)}, u32[]{:S(2)}) collective-permute-start(bf16[16,16,384]{2,1,0:T(8,128)(2,1)} %get-tuple-element.41), channel_id=1, source_target_pairs={{0,1},{1,2},{2,3},{3,4},{4,5},{5,6},{6,7},{7,8},{8,9},{9,10},{10,1... | collective-permute-start | bytes 589832 | tf_op jit(solution)/shard_map/ppermute | solution.py:444
  26.0 65.8 %collective-permute-start.7 = (bf16[16,16,384]{2,1,0:T(8,128)(2,1)}, bf16[16,16,384]{2,1,0:T(8,128)(2,1)S(1)}, u32[]{:S(2)}, u32[]{:S(2)}) collective-permute-start(bf16[16,16,384]{2,1,0:T(8,128)(2,1)} %get-tuple-element.42), channel_id=1, source_target_pairs={{0,2},{1,3},{2,4},{3,5},{4,6},{5,7},{6,8},{7,9},{8,10},{9,11},{10,... | collective-permute-start | bytes 589832 | tf_op jit(solution)/shard_map/ppermute | solution.py:444
  42.0 59.9 %collective-permute-start.8 = (bf16[16,16,384]{2,1,0:T(8,128)(2,1)}, bf16[16,16,384]{2,1,0:T(8,128)(2,1)S(1)}, u32[]{:S(2)}, u32[]{:S(2)}) collective-permute-start(bf16[16,16,384]{2,1,0:T(8,128)(2,1)} %get-tuple-element.43), channel_id=1, source_target_pairs={{0,3},{1,4},{2,5},{3,6},{4,7},{5,8},{6,9},{7,10},{8,11},{9,12},{10... | collective-permute-start | bytes 589832 | tf_op jit(solution)/shard_map/ppermute | solution.py:444
  58.4 45.5 %collective-permute-start.9 = (bf16[16,16,384]{2,1,0:T(8,128)(2,1)}, bf16[16,16,384]{2,1,0:T(8,128)(2,1)S(1)}, u32[]{:S(2)}, u32[]{:S(2)}) collective-permute-start(bf16[16,16,384]{2,1,0:T(8,128)(2,1)} %get-tuple-element.44), channel_id=1, source_target_pairs={{0,4},{1,5},{2,6},{3,7},{4,8},{5,9},{6,10},{7,11},{8,12},{9,13},{1... | collective-permute-start | bytes 589832 | tf_op jit(solution)/shard_map/ppermute | solution.py:444
  60.9 64.9 %collective-permute-start.10 = (bf16[16,16,384]{2,1,0:T(8,128)(2,1)}, bf16[16,16,384]{2,1,0:T(8,128)(2,1)S(1)}, u32[]{:S(2)}, u32[]{:S(2)}) collective-permute-start(bf16[16,16,384]{2,1,0:T(8,128)(2,1)} %get-tuple-element.45), channel_id=1, source_target_pairs={{0,5},{1,6},{2,7},{3,8},{4,9},{5,10},{6,11},{7,12},{8,13},{9,14},{... | collective-permute-start | bytes 589832 | tf_op jit(solution)/shard_map/ppermute | solution.py:444
  90.3 43.0 %copy-start.2 = (bf16[16,16,384]{2,1,0:T(8,128)(2,1)}, bf16[16,16,384]{2,1,0:T(8,128)(2,1)S(1)}, u32[]{:S(2)}) copy-start(bf16[16,16,384]{2,1,0:T(8,128)(2,1)S(1)} %collective-permute-done.6.refs_1_) | copy-start | bytes 589828
  90.3 35.6 %collective-permute-start.3 = (bf16[16,16,384]{2,1,0:T(8,128)(2,1)S(1)}, bf16[16,16,384]{2,1,0:T(8,128)(2,1)S(1)}, u32[]{:S(2)}, u32[]{:S(2)}) collective-permute-start(bf16[16,16,384]{2,1,0:T(8,128)(2,1)S(1)} %get-tuple-element.66), channel_id=1, source_target_pairs={{0,64},{16,80},{32,96},{48,112},{64,128},{80,144},{96,160},{112,17... | collective-permute-start | bytes 589832 | tf_op jit(solution)/shard_map/ppermute | solution.py:418
  91.7 41.5 %copy-start.3 = (bf16[16,16,384]{2,1,0:T(8,128)(2,1)}, bf16[16,16,384]{2,1,0:T(8,128)(2,1)S(1)}, u32[]{:S(2)}) copy-start(bf16[16,16,384]{2,1,0:T(8,128)(2,1)S(1)} %collective-permute-done.7.refs_2_) | copy-start | bytes 589828
  91.8 34.2 %collective-permute-start.5 = (bf16[16,16,384]{2,1,0:T(8,128)(2,1)S(1)}, bf16[16,16,384]{2,1,0:T(8,128)(2,1)S(1)}, u32[]{:S(2)}, u32[]{:S(2)}) collective-permute-start(bf16[16,16,384]{2,1,0:T(8,128)(2,1)S(1)} %get-tuple-element.67), channel_id=1, source_target_pairs={{0,128},{16,144},{32,160},{48,176},{64,192},{80,208},{96,224},{112... | collective-permute-start | bytes 589832 | tf_op jit(solution)/shard_map/ppermute | solution.py:418
  101.9 31.3 %copy-start.4 = (bf16[16,16,384]{2,1,0:T(8,128)(2,1)}, bf16[16,16,384]{2,1,0:T(8,128)(2,1)S(1)}, u32[]{:S(2)}) copy-start(bf16[16,16,384]{2,1,0:T(8,128)(2,1)S(1)} %collective-permute-done.8.refs_3_) | copy-start | bytes 589828
  101.9 29.7 %collective-permute-start.4 = (bf16[16,16,384]{2,1,0:T(8,128)(2,1)S(1)}, bf16[16,16,384]{2,1,0:T(8,128)(2,1)S(1)}, u32[]{:S(2)}, u32[]{:S(2)}) collective-permute-start(bf16[16,16,384]{2,1,0:T(8,128)(2,1)S(1)} %get-tuple-element.68), channel_id=1, source_target_pairs={{0,192},{16,208},{32,224},{48,240},{64,0},{80,16},{96,32},{112,48}... | collective-permute-start | bytes 589832 | tf_op jit(solution)/shard_map/ppermute | solution.py:418
  103.9 29.4 %copy-start.5 = (bf16[16,16,384]{2,1,0:T(8,128)(2,1)}, bf16[16,16,384]{2,1,0:T(8,128)(2,1)S(1)}, u32[]{:S(2)}) copy-start(bf16[16,16,384]{2,1,0:T(8,128)(2,1)S(1)} %collective-permute-done.9.refs_4_) | copy-start | bytes 589828
  103.9 29.5 %collective-permute-start.11 = (bf16[16,16,384]{2,1,0:T(8,128)(2,1)}, bf16[16,16,384]{2,1,0:T(8,128)(2,1)}, u32[]{:S(2)}, u32[]{:S(2)}) collective-permute-start(bf16[16,16,384]{2,1,0:T(8,128)(2,1)} %get-tuple-element.46), channel_id=1, source_target_pairs={{0,6},{1,7},{2,8},{3,9},{4,10},{5,11},{6,12},{7,13},{8,14},{9,15},... | collective-permute-start | bytes 589832 | tf_op jit(solution)/shard_map/ppermute | solution.py:444
  125.8 7.4 %copy-start.6 = (bf16[16,16,384]{2,1,0:T(8,128)(2,1)}, bf16[16,16,384]{2,1,0:T(8,128)(2,1)S(1)}, u32[]{:S(2)}) copy-start(bf16[16,16,384]{2,1,0:T(8,128)(2,1)S(1)} %collective-permute-done.10.refs_5_) | copy-start | bytes 589828
  125.8 18.4 %collective-permute-start.12 = (bf16[16,16,384]{2,1,0:T(8,128)(2,1)}, bf16[16,16,384]{2,1,0:T(8,128)(2,1)}, u32[]{:S(2)}, u32[]{:S(2)}) collective-permute-start(bf16[16,16,384]{2,1,0:T(8,128)(2,1)} %get-tuple-element.47), channel_id=1, source_target_pairs={{0,7},{1,8},{2,9},{3,10},{4,11},{5,12},{6,13},{7,14},{8,15},{9,0},... | collective-permute-start | bytes 589832 | tf_op jit(solution)/shard_map/ppermute | solution.py:444
  125.8 26.4 %collective-permute-start.13 = (bf16[16,16,384]{2,1,0:T(8,128)(2,1)}, bf16[16,16,384]{2,1,0:T(8,128)(2,1)}, u32[]{:S(2)}, u32[]{:S(2)}) collective-permute-start(bf16[16,16,384]{2,1,0:T(8,128)(2,1)} %get-tuple-element.48), channel_id=1, source_target_pairs={{0,8},{1,9},{2,10},{3,11},{4,12},{5,13},{6,14},{7,15},{8,0},{9,1},... | collective-permute-start | bytes 589832 | tf_op jit(solution)/shard_map/ppermute | solution.py:444
  126.0 37.4 %collective-permute-start.14 = (bf16[16,16,384]{2,1,0:T(8,128)(2,1)}, bf16[16,16,384]{2,1,0:T(8,128)(2,1)}, u32[]{:S(2)}, u32[]{:S(2)}) collective-permute-start(bf16[16,16,384]{2,1,0:T(8,128)(2,1)} %get-tuple-element.49), channel_id=1, source_target_pairs={{0,9},{1,10},{2,11},{3,12},{4,13},{5,14},{6,15},{7,0},{8,1},{9,2},... | collective-permute-start | bytes 589832 | tf_op jit(solution)/shard_map/ppermute | solution.py:444
  131.6 35.1 %collective-permute-start.15 = (bf16[16,16,384]{2,1,0:T(8,128)(2,1)}, bf16[16,16,384]{2,1,0:T(8,128)(2,1)}, u32[]{:S(2)}, u32[]{:S(2)}) collective-permute-start(bf16[16,16,384]{2,1,0:T(8,128)(2,1)} %get-tuple-element.50), channel_id=1, source_target_pairs={{0,10},{1,11},{2,12},{3,13},{4,14},{5,15},{6,0},{7,1},{8,2},{9,3},... | collective-permute-start | bytes 589832 | tf_op jit(solution)/shard_map/ppermute | solution.py:444
  133.4 33.3 %copy-start.1 = (bf16[16,16,16,384]{3,2,1,0:T(8,128)(2,1)}, bf16[16,16,16,384]{3,2,1,0:T(8,128)(2,1)S(1)}, u32[]{:S(2)}) copy-start(bf16[16,16,16,384]{3,2,1,0:T(8,128)(2,1)S(1)} %all-to-all-done.received) | copy-start | bytes 9437188
  133.4 52.2 %collective-permute-start.16 = (bf16[16,16,384]{2,1,0:T(8,128)(2,1)}, bf16[16,16,384]{2,1,0:T(8,128)(2,1)}, u32[]{:S(2)}, u32[]{:S(2)}) collective-permute-start(bf16[16,16,384]{2,1,0:T(8,128)(2,1)} %get-tuple-element.51), channel_id=1, source_target_pairs={{0,11},{1,12},{2,13},{3,14},{4,15},{5,0},{6,1},{7,2},{8,3},{9,4},{... | collective-permute-start | bytes 589832 | tf_op jit(solution)/shard_map/ppermute | solution.py:444
  144.3 41.4 %collective-permute-start.17 = (bf16[16,16,384]{2,1,0:T(8,128)(2,1)}, bf16[16,16,384]{2,1,0:T(8,128)(2,1)}, u32[]{:S(2)}, u32[]{:S(2)}) collective-permute-start(bf16[16,16,384]{2,1,0:T(8,128)(2,1)} %get-tuple-element.52), channel_id=1, source_target_pairs={{0,12},{1,13},{2,14},{3,15},{4,0},{5,1},{6,2},{7,3},{8,4},{9,5},{1... | collective-permute-start | bytes 589832 | tf_op jit(solution)/shard_map/ppermute | solution.py:444
  152.3 40.6 %collective-permute-start.18 = (bf16[16,16,384]{2,1,0:T(8,128)(2,1)}, bf16[16,16,384]{2,1,0:T(8,128)(2,1)}, u32[]{:S(2)}, u32[]{:S(2)}) collective-permute-start(bf16[16,16,384]{2,1,0:T(8,128)(2,1)} %get-tuple-element.53), channel_id=1, source_target_pairs={{0,13},{1,14},{2,15},{3,0},{4,1},{5,2},{6,3},{7,4},{8,5},{9,6},{10... | collective-permute-start | bytes 589832 | tf_op jit(solution)/shard_map/ppermute | solution.py:444
  163.3 29.9 %collective-permute-start.19 = (bf16[16,16,384]{2,1,0:T(8,128)(2,1)}, bf16[16,16,384]{2,1,0:T(8,128)(2,1)}, u32[]{:S(2)}, u32[]{:S(2)}) collective-permute-start(bf16[16,16,384]{2,1,0:T(8,128)(2,1)} %get-tuple-element.54), channel_id=1, source_target_pairs={{0,14},{1,15},{2,0},{3,1},{4,2},{5,3},{6,4},{7,5},{8,6},{9,7},{10,... | collective-permute-start | bytes 589832 | tf_op jit(solution)/shard_map/ppermute | solution.py:444
  166.7 29.5 %collective-permute-start.20 = (bf16[16,16,384]{2,1,0:T(8,128)(2,1)}, bf16[16,16,384]{2,1,0:T(8,128)(2,1)}, u32[]{:S(2)}, u32[]{:S(2)}) collective-permute-start(bf16[16,16,384]{2,1,0:T(8,128)(2,1)} %get-tuple-element.55), channel_id=1, source_target_pairs={{0,15},{1,0},{2,1},{3,2},{4,3},{5,4},{6,5},{7,6},{8,7},{9,8},{10,9... | collective-permute-start | bytes 589832 | tf_op jit(solution)/shard_map/ppermute | solution.py:444
  215.9 13.5 %collective-permute-start.21 = (bf16[4,8,16,384]{3,2,1,0:T(8,128)(2,1)}, bf16[4,8,16,384]{3,2,1,0:T(8,128)(2,1)S(1)}, u32[]{:S(2)}, u32[]{:S(2)}) collective-permute-start(bf16[4,8,16,384]{3,2,1,0:T(8,128)(2,1)} %get-tuple-element.58), channel_id=1, source_target_pairs={{0,16},{16,32},{32,48},{48,0},{64,80},{80,96},{96,112},{112,64},{1... | collective-permute-start | bytes 1179656 | tf_op jit(solution)/shard_map/ppermute | solution.py:418
  217.5 19.8 %collective-permute-start.22 = (bf16[4,8,16,384]{3,2,1,0:T(8,128)(2,1)}, bf16[4,8,16,384]{3,2,1,0:T(8,128)(2,1)S(1)}, u32[]{:S(2)}, u32[]{:S(2)}) collective-permute-start(bf16[4,8,16,384]{3,2,1,0:T(8,128)(2,1)} %get-tuple-element.59), channel_id=1, source_target_pairs={{0,48},{16,0},{32,16},{48,32},{64,112},{80,64},{96,80},{112,96},{1... | collective-permute-start | bytes 1179656 | tf_op jit(solution)/shard_map/ppermute | solution.py:418
  219.2 19.8 %collective-permute-start.23 = (bf16[4,8,16,384]{3,2,1,0:T(8,128)(2,1)}, bf16[4,8,16,384]{3,2,1,0:T(8,128)(2,1)S(1)}, u32[]{:S(2)}, u32[]{:S(2)}) collective-permute-start(bf16[4,8,16,384]{3,2,1,0:T(8,128)(2,1)} %get-tuple-element.60), channel_id=1, source_target_pairs={{0,32},{16,48},{32,0},{48,16},{64,96},{80,112},{96,64},{112,80},{1... | collective-permute-start | bytes 1179656 | tf_op jit(solution)/shard_map/ppermute | solution.py:418
  221.2 21.7 %collective-permute-start.27 = (bf16[4,8,16,384]{3,2,1,0:T(8,128)(2,1)}, bf16[4,8,16,384]{3,2,1,0:T(8,128)(2,1)S(1)}, u32[]{:S(2)}, u32[]{:S(2)}) collective-permute-start(bf16[4,8,16,384]{3,2,1,0:T(8,128)(2,1)} %get-tuple-element.62), channel_id=1, source_target_pairs={{0,64},{16,80},{32,96},{48,112},{64,128},{80,144},{96,160},{112,17... | collective-permute-start | bytes 1179656 | tf_op jit(solution)/shard_map/ppermute | solution.py:418
  222.7 22.4 %collective-permute-start.28 = (bf16[4,8,16,384]{3,2,1,0:T(8,128)(2,1)}, bf16[4,8,16,384]{3,2,1,0:T(8,128)(2,1)S(1)}, u32[]{:S(2)}, u32[]{:S(2)}) collective-permute-start(bf16[4,8,16,384]{3,2,1,0:T(8,128)(2,1)} %get-tuple-element.63), channel_id=1, source_target_pairs={{0,192},{16,208},{32,224},{48,240},{64,0},{80,16},{96,32},{112,48}... | collective-permute-start | bytes 1179656 | tf_op jit(solution)/shard_map/ppermute | solution.py:418
  229.4 15.7 %collective-permute-start.29 = (bf16[4,8,16,384]{3,2,1,0:T(8,128)(2,1)}, bf16[4,8,16,384]{3,2,1,0:T(8,128)(2,1)S(1)}, u32[]{:S(2)}, u32[]{:S(2)}) collective-permute-start(bf16[4,8,16,384]{3,2,1,0:T(8,128)(2,1)} %get-tuple-element.64), channel_id=1, source_target_pairs={{0,128},{16,144},{32,160},{48,176},{64,192},{80,208},{96,224},{112... | collective-permute-start | bytes 1179656 | tf_op jit(solution)/shard_map/ppermute | solution.py:418
  240.2 12.6 %collective-permute-start.24 = (bf16[8,16,384]{2,1,0:T(8,128)(2,1)S(1)}, bf16[8,16,384]{2,1,0:T(8,128)(2,1)S(1)}, u32[]{:S(2)}, u32[]{:S(2)}) collective-permute-start(bf16[8,16,384]{2,1,0:T(8,128)(2,1)S(1)} %get-tuple-element.69), channel_id=1, source_target_pairs={{0,64},{16,80},{32,96},{48,112},{64,128},{80,144},{96,160},{112,17... | collective-permute-start | bytes 294920 | tf_op jit(solution)/shard_map/ppermute | solution.py:418
  241.8 13.5 %collective-permute-start.26 = (bf16[8,16,384]{2,1,0:T(8,128)(2,1)S(1)}, bf16[8,16,384]{2,1,0:T(8,128)(2,1)S(1)}, u32[]{:S(2)}, u32[]{:S(2)}) collective-permute-start(bf16[8,16,384]{2,1,0:T(8,128)(2,1)S(1)} %get-tuple-element.70), channel_id=1, source_target_pairs={{0,128},{16,144},{32,160},{48,176},{64,192},{80,208},{96,224},{112... | collective-permute-start | bytes 294920 | tf_op jit(solution)/shard_map/ppermute | solution.py:418
  242.9 12.4 %collective-permute-start.25 = (bf16[8,16,384]{2,1,0:T(8,128)(2,1)S(1)}, bf16[8,16,384]{2,1,0:T(8,128)(2,1)S(1)}, u32[]{:S(2)}, u32[]{:S(2)}) collective-permute-start(bf16[8,16,384]{2,1,0:T(8,128)(2,1)S(1)} %get-tuple-element.71), channel_id=1, source_target_pairs={{0,192},{16,208},{32,224},{48,240},{64,0},{80,16},{96,32},{112,48}... | collective-permute-start | bytes 294920 | tf_op jit(solution)/shard_map/ppermute | solution.py:418
  246.3 9.1 %collective-permute-start.30 = (bf16[8,16,384]{2,1,0:T(8,128)(2,1)S(1)}, bf16[8,16,384]{2,1,0:T(8,128)(2,1)S(1)}, u32[]{:S(2)}, u32[]{:S(2)}) collective-permute-start(bf16[8,16,384]{2,1,0:T(8,128)(2,1)S(1)} %get-tuple-element.72), channel_id=1, source_target_pairs={{0,16},{16,32},{32,48},{48,0},{64,80},{80,96},{96,112},{112,64},{1... | collective-permute-start | bytes 294920 | tf_op jit(solution)/shard_map/ppermute | solution.py:418
  247.6 8.8 %collective-permute-start.32 = (bf16[8,16,384]{2,1,0:T(8,128)(2,1)S(1)}, bf16[8,16,384]{2,1,0:T(8,128)(2,1)S(1)}, u32[]{:S(2)}, u32[]{:S(2)}) collective-permute-start(bf16[8,16,384]{2,1,0:T(8,128)(2,1)S(1)} %get-tuple-element.73), channel_id=1, source_target_pairs={{0,32},{16,48},{32,0},{48,16},{64,96},{80,112},{96,64},{112,80},{1... | collective-permute-start | bytes 294920 | tf_op jit(solution)/shard_map/ppermute | solution.py:418
  252.8 4.7 %collective-permute-start.31 = (bf16[8,16,384]{2,1,0:T(8,128)(2,1)S(1)}, bf16[8,16,384]{2,1,0:T(8,128)(2,1)S(1)}, u32[]{:S(2)}, u32[]{:S(2)}) collective-permute-start(bf16[8,16,384]{2,1,0:T(8,128)(2,1)S(1)} %get-tuple-element.74), channel_id=1, source_target_pairs={{0,48},{16,0},{32,16},{48,32},{64,112},{80,64},{96,80},{112,96},{1... | collective-permute-start | bytes 294920 | tf_op jit(solution)/shard_map/ppermute | solution.py:418
  287.5 75.5 %all-to-all-start.1 = ((bf16[16,16,16,384]{3,2,1,0:T(8,128)(2,1)}), bf16[16,16,16,384]{3,2,1,0:T(8,128)(2,1)S(1)}, u32[]{:S(2)}, u32[]{:S(2)}) async-start(bf16[16,16,16,384]{3,2,1,0:T(8,128)(2,1)} %get-tuple-element.39), calls=%async_computation.1 | async-start | bytes 6291456 | tf_op jit(solution)/shard_map/all_to_all | solution.py:449
  363.0 1.6 copy-start

commit v3 on v2

--- a/solution.py
+++ b/solution.py
@@ -1,3 +1,4 @@
+import functools
 import math
 
 import jax
@@ -83,21 +84,21 @@
         put_rows(out, (i, j), dot(table[...], summed))
 
 
-def rows_cot_kernel(me, here, table, cot, *rest):
-    outs, pieces, ordered = rest[:N], rest[N : N + 4], rest[N + 4]
+def rows_cot_kernel(distances, me, here, table, cot, *rest):
+    outs, pieces, ordered = rest[: len(distances)], rest[len(distances) : -1], rest[-1]
 
     @pl.when(pl.program_id(0) == 0)
     def _():
-        for j in range(N):
+        for at, j in enumerate(distances):
             owner = (here[0] + j) & (N - 1)
-            ordered[j * 16 : (j + 1) * 16] = table[pl.ds(pl.multiple_of(owner * 16, 16), 16), :]
+            ordered[at * 16 : (at + 1) * 16] = table[pl.ds(pl.multiple_of(owner * 16, 16), 16), :]
 
     for i, j in PAIRS:
         value = dot(ordered[...], beside(cot[i], cot[j])).astype(BF)
-        for step in range(N):
-            part = value[step * 16 : (step + 1) * 16]
-            outs[step][i] = part[:, :C]
-            outs[step][j] = part[:, C:]
+        for at in range(len(distances)):
+            part = value[at * 16 : (at + 1) * 16]
+            outs[at][i] = part[:, :C]
+            outs[at][j] = part[:, C:]
 
     x, y = me[0] >> 2, me[0] & 3
 
@@ -109,7 +110,8 @@
                 pieces[a][b, i] = cot[i, rows, :]
         return carry
 
-    lax.fori_loop(0, 4, slot, 0)
+    if pieces:
+        lax.fori_loop(0, 4, slot, 0)
 
 
 GRID_SPEC = pl.BlockSpec((HB, W, C), lambda i: (i, 0, 0))
@@ -133,17 +135,24 @@
     )(ROW_FWD, scene, prompt)
 
 
-def rows_cot(me, here, cot):
-    return pl.pallas_call(
-        rows_cot_kernel,
+SEND_ORDER = (8, 7, 9, 6, 10, 5, 11, 4, 12, 3, 13, 2, 14, 1, 15)
+EARLY = 4
+
+
+def rows_cot(me, here, cot, distances, with_pieces):
+    count = len(distances)
+    pieces = 4 if with_pieces else 0
+    return pl.pallas_call(
+        functools.partial(rows_cot_kernel, distances),
         grid=(N // HB,),
         in_specs=[ME_SPEC, ME_SPEC, full((W, W)), GRID_SPEC],
-        out_specs=[pl.BlockSpec((HB, 16, C), lambda i: (i, 0, 0))] * N
-        + [pl.BlockSpec((4, HB, 16, C), lambda i: (0, i, 0, 0))] * 4,
-        out_shape=[jax.ShapeDtypeStruct((N, 16, C), BF)] * N + [jax.ShapeDtypeStruct((4, N, 16, C), BF)] * 4,
-        scratch_shapes=[pltpu.VMEM((W, W), BF)],
-        cost_estimate=cost(ROW_FLOPS, 3 * ARRAY_BYTES),
-        name="rows_cot",
+        out_specs=[pl.BlockSpec((HB, 16, C), lambda i: (i, 0, 0))] * count
+        + [pl.BlockSpec((4, HB, 16, C), lambda i: (0, i, 0, 0))] * pieces,
+        out_shape=[jax.ShapeDtypeStruct((N, 16, C), BF)] * count
+        + [jax.ShapeDtypeStruct((4, N, 16, C), BF)] * pieces,
+        scratch_shapes=[pltpu.VMEM((16 * count, W), BF)],
+        cost_estimate=cost(ROW_FLOPS * count // N, ARRAY_BYTES * (N + count + 4 * pieces) // N),
+        name="rows_cot_late" if with_pieces else "rows_cot_early",
     )(me, here, ROW_INV, cot)
 
 
@@ -435,14 +444,8 @@
     return shifted_sum([along[i] for i in range(4)], along_x)
 
 
-SEND_ORDER = (8, 7, 9, 6, 10, 5, 11, 4, 12, 3, 13, 2, 14, 1, 15)
-
-
-def send_round(pieces):
-    received = {0: pieces[0]}
-    for j in SEND_ORDER:
-        received[j] = lax.ppermute(pieces[j], "rows", [(i, (i + j) % N) for i in range(N)])
-    return [received[j] for j in range(N)]
+def send_round(pieces, order):
+    return {j: lax.ppermute(pieces[j], "rows", [(i, (i + j) % N) for i in range(N)]) for j in order}
 
 
 def exchange(blocks, axis):
@@ -455,10 +458,16 @@
     w2 = second_weight.reshape(2, C, BS)
     here = lax.axis_index("rows").reshape(1)
     me = lax.axis_index("dp").reshape(1)
-    scene_cols = exchange(rows_scene(scene, prompt), "rows")
-    leaving = rows_cot(me, here, cot)
-    cot_sum = plain_sum_over_dp(leaving[N:])
-    cot_cols = send_round(leaving[:N])
+    early, late = SEND_ORDER[:EARLY], (0,) + SEND_ORDER[EARLY:]
+    first = rows_cot(me, here, cot, early, False)
+    late_scene, *first = lax.optimization_barrier((scene, *first))
+    scene_cols = exchange(rows_scene(late_scene, prompt), "rows")
+    last = rows_cot(me, here, cot, late, True)
+    cot_sum = plain_sum_over_dp(last[len(late) :])
+    last = dict(zip(late, last))
+    arrived = send_round(dict(zip(early, first)), early)
+    arrived |= send_round(last, late[1:]) | {0: last[0]}
+    cot_cols = [arrived[j] for j in range(N)]
     scene_cols, cot_sum = lax.optimization_barrier((scene_cols, cot_sum))
     mixed_cols, slope = mix(scene_cols, w1, first_bias, w2, second_bias)
     mixed_rows = exchange(mixed_cols, "rows")

time: 374 us -> 363 us (0.971)
  waiting for transfers between devices: 198 us -> 175 us
  starting transfers between devices: 78.7 us -> 84 us
  Pallas kernels: 59.5 us -> 63.5 us
    ppermute x15, waiting for transfers between devices: 81.7 us -> 64.5 us  [send_round(): lax.ppermute(pieces[j], 'rows', [(i, (i + j) % N) for i in range(N)])]
    ppermute x15, starting transfers between devices: 34 us -> 39.5 us  [send_round(): lax.ppermute(pieces[j], 'rows', [(i, (i + j) % N) for i in range(N)])]
    ppermute x18, waiting for transfers between devices: 45.8 us -> 40.9 us  [shifted_sum(): received = [lax.ppermute(pieces[j], 'dp', perm_of(j)) for j in (1, 3, 2)]]
    pallas_call x1 -> x2, Pallas kernels: 5.85 us -> 9.79 us  [rows_cot(): pl.pallas_call(functools.partial(rows_cot_kernel, distances), grid=(N //...]
  transfers between devices with their start and end apart: 35 -> 35, of which waited for: 18 -> 14; matrix products, arithmetic and copies ran while one was open for 2% -> 2% of each run, Pallas kernels for 7% -> 7%
where the time goes in v3:
time: 363 us; the launch traced here: 361 us
  waiting for transfers between devices  175 us (48%)
  starting transfers between devices  84 us (23%)
  Pallas kernels  63.5 us (17%)
  blocking collectives  29.4 us (8%)
  other arithmetic  5.89 us (2%)
    all_to_all x2, waiting for transfers between devices, exchange(): return lax.all_to_all(blocks, axis, split_axis=0, concat_axis=0, tiled=True)  70 us
    ppermute x15, waiting for transfers between devices, send_round(): lax.ppermute(pieces[j], 'rows', [(i, (i + j) % N) for i in range(N)])  64.5 us
    ppermute x18, waiting for transfers between devices, shifted_sum(): received = [lax.ppermute(pieces[j], 'dp', perm_of(j)) for j in (1, 3, 2)]  40.9 us
    ppermute x15, starting transfers between devices, send_round(): lax.ppermute(pieces[j], 'rows', [(i, (i + j) % N) for i in range(N)])  39.5 us
    ppermute x18, starting transfers between devices, shifted_sum(): received = [lax.ppermute(pieces[j], 'dp', perm_of(j)) for j in (1, 3, 2)]  32.2 us
    all_to_all x2, blocking collectives, exchange(): return lax.all_to_all(blocks, axis, split_axis=0, concat_axis=0, tiled=True)  29.4 us
    pallas_call x1, Pallas kernels, back(): pl.pallas_call(back_kernel, grid=(K8 // 2,), in_specs=[ME_SPEC, ME_SPEC,...  19.8 us
    pallas_call x1, Pallas kernels, mix(): pl.pallas_call(mix_kernel, grid=(K8 // 2,), in_specs=[FULL_SPEC, full((2,...  18.9 us
  transfers between devices with their start and end apart: 35, of which 14 were waited for; matrix products, arithmetic and copies ran while one was open for 2% of the time, Pallas kernels for 7%

profile of v3, /device:TPU:2, one launch (start us, length us, event | category | flops | bytes accessed | tf_op | source)
XLA Modules:
  0.0 360.9 jit_solution(7435840369176911948)
XLA Ops:
  0.6 4.2 %rows_cot_early.1 = (bf16[16,16,384]{2,1,0:T(8,128)(2,1)}, bf16[16,16,384]{2,1,0:T(8,128)(2,1)}, bf16[16,16,384]{2,1,0:T(8,128)(2,1)}, bf16[16,16,384]{2,1,0:T(8,128)(2,1)}) custom-call(s32[1]{0:T(128)} %bitcast.1.me, s32[1]{0:T(128)} %bitcast.2.here, bf16[256,256]{1,0:T(8,128)(2,1)} %constant.17.clone.table, bf16[16,256,384]{2,1,0:T(8,128)(2,1)} %bitcast.43), custom_call_target="tpu_custom_call" | custom-call | flops 201326592 | bytes 3932160 | tf_op jit(solution)/shard_map/rows_cot_early/pallas_call | solution.py:145
  4.9 5.6 %rows_scene.1 = bf16[16,16,16,384]{3,2,1,0:T(8,128)(2,1)} custom-call(bf16[256,256]{1,0:T(8,128)(2,1)} %constant.18.clone.table, bf16[16,256,384]{2,1,0:T(8,128)(2,1)} %bitcast.40, bf16[16,256,384]{2,1,0:T(8,128)(2,1)} %prompt.5), custom_call_target="tpu_custom_call" | custom-call | flops 805306368 | bytes 9437184 | tf_op jit(solution)/shard_map/rows_scene/pallas_call | solution.py:127
  10.5 8.6 %all-to-all-start = ((bf16[16,16,16,384]{3,2,1,0:T(8,128)(2,1)}), bf16[16,16,16,384]{3,2,1,0:T(8,128)(2,1)S(1)}, u32[]{:S(2)}, u32[]{:S(2)}) async-start(bf16[16,16,16,384]{3,2,1,0:T(8,128)(2,1)} %rows_scene.1), calls=%async_computation | async-start | bytes 6291456 | tf_op jit(solution)/shard_map/all_to_all | solution.py:452
  19.0 5.6 %rows_cot_late.1 = (bf16[16,16,384]{2,1,0:T(8,128)(2,1)}, bf16[16,16,384]{2,1,0:T(8,128)(2,1)}, bf16[16,16,384]{2,1,0:T(8,128)(2,1)}, bf16[16,16,384]{2,1,0:T(8,...) custom-call(s32[1]{0:T(128)} %bitcast.1.me, ...), custom_call_target="tpu_custom_call" | custom-call | flops 603979776 | bytes 8650752 | tf_op jit(solution)/shard_map/rows_cot_late/pallas_call | solution.py:145
  24.6 1.7 collective-permute-start
  26.3 1.7 collective-permute-start.1
  27.9 2.0 collective-permute-start.2
  29.9 3.7 %collective-permute-start.11 = (bf16[16,16,384]{2,1,0:T(8,128)(2,1)}, bf16[16,16,384]{2,1,0:T(8,128)(2,1)S(1)}, u32[]{:S(2)}, u32[]{:S(2)}) collective-permute-start(bf16[16,16,384]{2,1,0:T(8,128)(2,1)} %get-tuple-element.56), channel_id=1, source_target_pairs={{0,6},{1,7},{2,8},{3,9},{4,10},{5,11},{6,12},{7,13},{8,14},{9,15},... | collective-permute-start | bytes 589832 | tf_op jit(solution)/shard_map/ppermute | solution.py:448
  33.6 1.3 collective-permute-start.12
  34.9 11.1 %collective-permute-done = bf16[4,16,16,384]{3,2,1,0:T(8,128)(2,1)S(1)} collective-permute-done((bf16[4,16,16,384]{3,2,1,0:T(8,128)(2,1)}, bf16[4,16,16,384]{3,2,1,0:T(8,128)(2,1)S(1)}, u32[]{:S(2)}, u32[]{:S(2)}) %collective-permute-start) | collective-permute-done | bytes 786464 | tf_op jit(solution)/shard_map/ppermute | solution.py:427
  46.0 5.5 %collective-permute-start.13 = (bf16[16,16,384]{2,1,0:T(8,128)(2,1)}, bf16[16,16,384]{2,1,0:T(8,128)(2,1)S(1)}, u32[]{:S(2)}, u32[]{:S(2)}) collective-permute-start(bf16[16,16,384]{2,1,0:T(8,128)(2,1)} %get-tuple-element.58), channel_id=1, source_target_pairs={{0,8},{1,9},{2,10},{3,11},{4,12},{5,13},{6,14},{7,15},{8,0},{9,1},... | collective-permute-start | bytes 589832 | tf_op jit(solution)/shard_map/ppermute | solution.py:448
  51.5 10.8 %collective-permute-done.1 = bf16[4,16,16,384]{3,2,1,0:T(8,128)(2,1)S(1)} collective-permute-done((bf16[4,16,16,384]{3,2,1,0:T(8,128)(2,1)}, bf16[4,16,16,384]{3,2,1,0:T(8,128)(2,1)S(1)}, u32[]{:S(2)}, u32[]{:S(2)}) %collective-permute-start.1) | collective-permute-done | bytes 786464 | tf_op jit(solution)/shard_map/ppermute | solution.py:427
  62.3 1.7 collective-permute-done.2
  64.0 3.1 collective-permute-start.6
  67.1 1.6 add_convert_fusion
  68.7 0.1 slice_bitcast_fusion.2
  68.7 37.2 %collective-permute-done.11.refs_6_ = bf16[16,16,384]{2,1,0:T(8,128)(2,1)S(1)} collective-permute-done((bf16[16,16,384]{2,1,0:T(8,128)(2,1)}, bf16[16,16,384]{2,1,0:T(8,128)(2,1)S(1)}, u32[]{:S(2)}, u32[]{:S(2)}) %collective-permute-start.11) | collective-permute-done | bytes 196640 | tf_op jit(solution)/shard_map/ppermute | solution.py:448
  105.9 1.5 collective-permute-start.3
  107.4 5.6 %collective-permute-done.12.refs_7_ = bf16[16,16,384]{2,1,0:T(8,128)(2,1)S(1)} collective-permute-done((bf16[16,16,384]{2,1,0:T(8,128)(2,1)}, bf16[16,16,384]{2,1,0:T(8,128)(2,1)S(1)}, u32[]{:S(2)}, u32[]{:S(2)}) %collective-permute-start.12) | collective-permute-done | bytes 196640 | tf_op jit(solution)/shard_map/ppermute | solution.py:448
  113.1 2.1 collective-permute-start.5
  115.2 7.1 %collective-permute-done.13.refs_8_ = bf16[16,16,384]{2,1,0:T(8,128)(2,1)S(1)} collective-permute-done((bf16[16,16,384]{2,1,0:T(8,128)(2,1)}, bf16[16,16,384]{2,1,0:T(8,128)(2,1)S(1)}, u32[]{:S(2)}, u32[]{:S(2)}) %collective-permute-start.13) | collective-permute-done | bytes 196640 | tf_op jit(solution)/shard_map/ppermute | solution.py:448
  122.3 0.5 collective-permute-start.4
  122.9 3.8 %collective-permute-start.7 = (bf16[16,16,384]{2,1,0:T(8,128)(2,1)}, bf16[16,16,384]{2,1,0:T(8,128)(2,1)}, u32[]{:S(2)}, u32[]{:S(2)}) collective-permute-start(bf16[16,16,384]{2,1,0:T(8,128)(2,1)} %get-tuple-element.52), channel_id=1, source_target_pairs={{0,2},{1,3},{2,4},{3,5},{4,6},{5,7},{6,8},{7,9},{8,10},{9,11},{10,... | collective-permute-start | bytes 589832 | tf_op jit(solution)/shard_map/ppermute | solution.py:448
  126.7 4.6 %collective-permute-start.8 = (bf16[16,16,384]{2,1,0:T(8,128)(2,1)}, bf16[16,16,384]{2,1,0:T(8,128)(2,1)}, u32[]{:S(2)}, u32[]{:S(2)}) collective-permute-start(bf16[16,16,384]{2,1,0:T(8,128)(2,1)} %get-tuple-element.53), channel_id=1, source_target_pairs={{0,3},{1,4},{2,5},{3,6},{4,7},{5,8},{6,9},{7,10},{8,11},{9,12},{10... | collective-permute-start | bytes 589832 | tf_op jit(solution)/shard_map/ppermute | solution.py:448
  131.3 1.2 collective-permute-start.9
  132.4 2.1 collective-permute-start.10
  134.6 2.3 collective-permute-start.15
  136.9 0.1 fusion.1
  137.1 6.4 %collective-permute-start.16 = (bf16[16,16,384]{2,1,0:T(8,128)(2,1)}, bf16[16,16,384]{2,1,0:T(8,128)(2,1)}, u32[]{:S(2)}, u32[]{:S(2)}) collective-permute-start(bf16[16,16,384]{2,1,0:T(8,128)(2,1)} %get-tuple-element.61), channel_id=1, source_target_pairs={{0,11},{1,12},{2,13},{3,14},{4,15},{5,0},{6,1},{7,2},{8,3},{9,4},{... | collective-permute-start | bytes 589832 | tf_op jit(solution)/shard_map/ppermute | solution.py:448
  143.5 2.3 collective-permute-done.9.refs_4_
  145.8 5.4 %collective-permute-start.18 = (bf16[16,16,384]{2,1,0:T(8,128)(2,1)}, bf16[16,16,384]{2,1,0:T(8,128)(2,1)}, u32[]{:S(2)}, u32[]{:S(2)}) collective-permute-start(bf16[16,16,384]{2,1,0:T(8,128)(2,1)} %get-tuple-element.63), channel_id=1, source_target_pairs={{0,13},{1,14},{2,15},{3,0},{4,1},{5,2},{6,3},{7,4},{8,5},{9,6},{10... | collective-permute-start | bytes 589832 | tf_op jit(solution)/shard_map/ppermute | solution.py:448
  151.3 12.2 %collective-permute-done.10.refs_5_ = bf16[16,16,384]{2,1,0:T(8,128)(2,1)} collective-permute-done((bf16[16,16,384]{2,1,0:T(8,128)(2,1)}, bf16[16,16,384]{2,1,0:T(8,128)(2,1)}, u32[]{:S(2)}, u32[]{:S(2)}) %collective-permute-start.10) | collective-permute-done | bytes 196640 | tf_op jit(solution)/shard_map/ppermute | solution.py:448
  163.5 18.9 %mix.1 = (bf16[16,16,16,384]{3,2,1,0:T(8,128)(2,1)}, f32[8,256,768]{2,1,0:T(8,128)}) custom-call(bf16[16,16,16,384]{3,2,1,0:T(8,128)(2,1)} %copy-done.1, bf16[2,256,256]{2,1,0:T(8,128)(2,1)} %constant.19.clone.col.refs_17_, bf16[2,384,48]{2,1,0:T(8,128)(2,1)} %bitcast.46, f32[2,384]{1,0:T(2,128)} %b1.1, bf16[2,384,48]{2,1,0:T(8,128)(2,1)} %bitcast.48, ...), custom_call_target="tpu_custom_call" | custom-call | flops 8053063680 | bytes 12582912 | tf_op jit(solution)/shard_map/mix/pallas_call | solution.py:330
  182.5 19.8 %back.1 = (bf16[4,8,16,384]{3,2,1,0:T(8,128)(2,1)}, bf16[4,8,16,384]{3,2,1,0:T(8,128)(2,1)}, bf16[4,8,16,384]{3,2,1,0:T(8,128)(2,1)}, bf16[4,8,16,384]{3,2,1,0:T...) custom-call(s32[1]{0:T(128)} %bitcast.1.me, ...), custom_call_target="tpu_custom_call" | custom-call | flops 8053063680 | bytes 12582912 | tf_op jit(solution)/shard_map/back/pallas_call | solution.py:352
  202.3 1.7 collective-permute-start.21
  203.9 1.7 collective-permute-start.22
  205.7 1.9 collective-permute-start.23
  207.6 1.0 collective-permute-start.27
  208.5 1.1 collective-permute-start.28
  209.6 6.0 %collective-permute-done.21 = bf16[4,8,16,384]{3,2,1,0:T(8,128)(2,1)S(1)} collective-permute-done((bf16[4,8,16,384]{3,2,1,0:T(8,128)(2,1)}, bf16[4,8,16,384]{3,2,1,0:T(8,128)(2,1)S(1)}, u32[]{:S(2)}, u32[]{:S(2)}) %collective-permute-start.21) | collective-permute-done | bytes 393248 | tf_op jit(solution)/shard_map/ppermute | solution.py:427
  215.6 0.4 collective-permute-start.29
  216.0 7.7 %collective-permute-done.22 = bf16[4,8,16,384]{3,2,1,0:T(8,128)(2,1)S(1)} collective-permute-done((bf16[4,8,16,384]{3,2,1,0:T(8,128)(2,1)}, bf16[4,8,16,384]{3,2,1,0:T(8,128)(2,1)S(1)}, u32[]{:S(2)}, u32[]{:S(2)}) %collective-permute-start.22) | collective-permute-done | bytes 393248 | tf_op jit(solution)/shard_map/ppermute | solution.py:427
  223.7 1.5 collective-permute-done.23
  225.2 1.2 add_convert_fusion.2
  226.4 1.2 collective-permute-start.24
  227.6 1.9 collective-permute-start.26
  229.6 0.2 collective-permute-start.25
  229.8 1.2 add_convert_fusion.1
  231.1 1.6 collective-permute-start.30
  232.7 7.4 %collective-permute-start.32 = (bf16[8,16,384]{2,1,0:T(8,128)(2,1)S(1)}, bf16[8,16,384]{2,1,0:T(8,128)(2,1)S(1)}, u32[]{:S(2)}, u32[]{:S(2)}) collective-permute-start(bf16[8,16,384]{2,1,0:T(8,128)(2,1)S(1)} %get-tuple-element.83), channel_id=1, source_target_pairs={{0,32},{16,48},{32,0},{48,16},{64,96},{80,112},{96,64},{112,80},{1... | collective-permute-start | bytes 294920 | tf_op jit(solution)/shard_map/ppermute | solution.py:427
  240.1 2.5 collective-permute-start.31
  242.7 0.1 fusion.7
  242.7 0.9 collective-permute-done.32
  243.7 1.2 collective-permute-done.31
  244.9 0.1 fusion.4
  245.0 14.8 %all_to_all.20.spec = bf16[16,16,384]{2,1,0:T(8,128)(2,1)} all-to-all(bf16[16,16,384]{2,1,0:T(8,128)(2,1)S(1)} %pad_maximum_fusion), channel_id=1, replica_groups=mesh['dp'=16,'rows'=16] {'rows'}, dimensions={0} | all-to-all | bytes 393216 | tf_op jit(solution)/shard_map/all_to_all | solution.py:452
  259.8 1.9 grad_row.1
  261.7 14.6 %all_to_all.21 = bf16[16,16,384]{2,1,0:T(8,128)(2,1)} all-to-all(bf16[16,16,384]{2,1,0:T(8,128)(2,1)} %grad_row.1), channel_id=1, replica_groups=mesh['dp'=16,'rows'=16] {'dp'}, dimensions={0} | all-to-all | bytes 393216 | tf_op jit(solution)/shard_map/all_to_all | solution.py:452
  276.3 3.7 %all-to-all-start.1 = ((bf16[16,16,16,384]{3,2,1,0:T(8,128)(2,1)}), bf16[16,16,16,384]{3,2,1,0:T(8,128)(2,1)S(1)}, u32[]{:S(2)}, u32[]{:S(2)}) async-start(bf16[16,16,16,384]{3,2,1,0:T(8,128)(2,1)} %get-tuple-element.49), calls=%async_computation.1 | async-start | bytes 6291456 | tf_op jit(solution)/shard_map/all_to_all | solution.py:452
  280.1 1.7 convert_add_fusion.1
  281.8 70.0 %all-to-all-done.1.spec = bf16[16,16,16,384]{3,2,1,0:T(8,128)(2,1)S(1)} async-done(((bf16[16,16,16,384]{3,2,1,0:T(8,128)(2,1)}), bf16[16,16,16,384]{3,2,1,0:T(8,128)(2,1)S(1)}, u32[]{:S(2)}, u32[]{:S(2)}) %all-to-all-start.1) | async-done | bytes 3145760 | tf_op jit(solution)/shard_map/all_to_all | solution.py:452
  351.8 1.6 copy-done
  353.4 3.7 %finish_a.1.rest_0_ = bf16[16,256,384]{2,1,0:T(8,128)(2,1)} custom-call(bf16[256,256]{1,0:T(8,128)(2,1)} %constant.17.clone.table, bf16[16,16,16,384]{3,2,1,0:T(8,128)(2,1)} %copy-done, bf16[16,256,384]{2,1,0:T(8,128)(2,1)} %bitcast.41, bf16[16,256,384]{2,1,0:T(8,128)(2,1)} %prompt.5), custom_call_target="tpu_custom_call" | custom-call | flops 402653184 | bytes 6291456 | tf_op jit(solution)/shard_map/finish_a/pallas_call | solution.py:390
  357.1 3.7 %finish_b.1 = bf16[16,256,384]{2,1,0:T(8,128)(2,1)} custom-call(bf16[256,256]{1,0:T(8,128)(2,1)} %constant.17.clone.table, bf16[16,16,16,384]{3,2,1,0:T(8,128)(2,1)} %copy-done, bf16[16,256,384]{2,1,0:T(8,128)(2,1)} %bitcast.42, bf16[16,256,384]{2,1,0:T(8,128)(2,1)} %prompt.5, bf16[16,256,384]{2,1,0:T(8,128)(2,1)} %finish_a.1.rest_0_), custom_call_target="tpu_custom_call", output_to_operand_aliasing={{}: (4, {})} | custom-call | flops 402653184 | bytes 6291456 | tf_op jit(solution)/shard_map/finish_b/pallas_call | solution.py:390
  (41 shorter events, 0.2 us)
Async XLA Ops:
  10.5 126.6 %all-to-all-start = ((bf16[16,16,16,384]{3,2,1,0:T(8,128)(2,1)}), bf16[16,16,16,384]{3,2,1,0:T(8,128)(2,1)S(1)}, u32[]{:S(2)}, u32[]{:S(2)}) async-start(bf16[16,16,16,384]{3,2,1,0:T(8,128)(2,1)} %rows_scene.1), calls=%async_computation | async-start | bytes 6291456 | tf_op jit(solution)/shard_map/all_to_all | solution.py:452
  24.6 21.4 %collective-permute-start = (bf16[4,16,16,384]{3,2,1,0:T(8,128)(2,1)}, bf16[4,16,16,384]{3,2,1,0:T(8,128)(2,1)S(1)}, u32[]{:S(2)}, u32[]{:S(2)}) collective-permute-start(bf16[4,16,16,384]{3,2,1,0:T(8,128)(2,1)} %get-tuple-element.45), channel_id=1, source_target_pairs={{0,16},{16,32},{32,48},{48,0},{64,80},{80,96},{96,112},{112,64},{1... | collective-permute-start | bytes 2359304 | tf_op jit(solution)/shard_map/ppermute | solution.py:427
  26.3 36.1 %collective-permute-start.1 = (bf16[4,16,16,384]{3,2,1,0:T(8,128)(2,1)}, bf16[4,16,16,384]{3,2,1,0:T(8,128)(2,1)S(1)}, u32[]{:S(2)}, u32[]{:S(2)}) collective-permute-start(bf16[4,16,16,384]{3,2,1,0:T(8,128)(2,1)} %get-tuple-element.46), channel_id=1, source_target_pairs={{0,48},{16,0},{32,16},{48,32},{64,112},{80,64},{96,80},{112,96},{1... | collective-permute-start | bytes 2359304 | tf_op jit(solution)/shard_map/ppermute | solution.py:427
  27.9 36.1 %collective-permute-start.2 = (bf16[4,16,16,384]{3,2,1,0:T(8,128)(2,1)}, bf16[4,16,16,384]{3,2,1,0:T(8,128)(2,1)S(1)}, u32[]{:S(2)}, u32[]{:S(2)}) collective-permute-start(bf16[4,16,16,384]{3,2,1,0:T(8,128)(2,1)} %get-tuple-element.47), channel_id=1, source_target_pairs={{0,32},{16,48},{32,0},{48,16},{64,96},{80,112},{96,64},{112,80},{1... | collective-permute-start | bytes 2359304 | tf_op jit(solution)/shard_map/ppermute | solution.py:427
  29.9 76.0 %collective-permute-start.11 = (bf16[16,16,384]{2,1,0:T(8,128)(2,1)}, bf16[16,16,384]{2,1,0:T(8,128)(2,1)S(1)}, u32[]{:S(2)}, u32[]{:S(2)}) collective-permute-start(bf16[16,16,384]{2,1,0:T(8,128)(2,1)} %get-tuple-element.56), channel_id=1, source_target_pairs={{0,6},{1,7},{2,8},{3,9},{4,10},{5,11},{6,12},{7,13},{8,14},{9,15},... | collective-permute-start | bytes 589832 | tf_op jit(solution)/shard_map/ppermute | solution.py:448
  33.6 79.5 %collective-permute-start.12 = (bf16[16,16,384]{2,1,0:T(8,128)(2,1)}, bf16[16,16,384]{2,1,0:T(8,128)(2,1)S(1)}, u32[]{:S(2)}, u32[]{:S(2)}) collective-permute-start(bf16[16,16,384]{2,1,0:T(8,128)(2,1)} %get-tuple-element.57), channel_id=1, source_target_pairs={{0,7},{1,8},{2,9},{3,10},{4,11},{5,12},{6,13},{7,14},{8,15},{9,0},... | collective-permute-start | bytes 589832 | tf_op jit(solution)/shard_map/ppermute | solution.py:448
  46.0 76.3 %collective-permute-start.13 = (bf16[16,16,384]{2,1,0:T(8,128)(2,1)}, bf16[16,16,384]{2,1,0:T(8,128)(2,1)S(1)}, u32[]{:S(2)}, u32[]{:S(2)}) collective-permute-start(bf16[16,16,384]{2,1,0:T(8,128)(2,1)} %get-tuple-element.58), channel_id=1, source_target_pairs={{0,8},{1,9},{2,10},{3,11},{4,12},{5,13},{6,14},{7,15},{8,0},{9,1},... | collective-permute-start | bytes 589832 | tf_op jit(solution)/shard_map/ppermute | solution.py:448
  62.3 60.5 %collective-permute-start.14 = (bf16[16,16,384]{2,1,0:T(8,128)(2,1)}, bf16[16,16,384]{2,1,0:T(8,128)(2,1)S(1)}, u32[]{:S(2)}, u32[]{:S(2)}) collective-permute-start(bf16[16,16,384]{2,1,0:T(8,128)(2,1)} %get-tuple-element.59), channel_id=1, source_target_pairs={{0,9},{1,10},{2,11},{3,12},{4,13},{5,14},{6,15},{7,0},{8,1},{9,2},... | collective-permute-start | bytes 589832 | tf_op jit(solution)/shard_map/ppermute | solution.py:448
  64.0 62.7 %collective-permute-start.6 = (bf16[16,16,384]{2,1,0:T(8,128)(2,1)}, bf16[16,16,384]{2,1,0:T(8,128)(2,1)S(1)}, u32[]{:S(2)}, u32[]{:S(2)}) collective-permute-start(bf16[16,16,384]{2,1,0:T(8,128)(2,1)} %get-tuple-element.51), channel_id=1, source_target_pairs={{0,1},{1,2},{2,3},{3,4},{4,5},{5,6},{6,7},{7,8},{8,9},{9,10},{10,1... | collective-permute-start | bytes 589832 | tf_op jit(solution)/shard_map/ppermute | solution.py:448
  105.9 31.0 %copy-start.2 = (bf16[16,16,384]{2,1,0:T(8,128)(2,1)}, bf16[16,16,384]{2,1,0:T(8,128)(2,1)S(1)}, u32[]{:S(2)}) copy-start(bf16[16,16,384]{2,1,0:T(8,128)(2,1)S(1)} %collective-permute-done.11.refs_6_) | copy-start | bytes 589828
  105.9 25.3 %collective-permute-start.3 = (bf16[16,16,384]{2,1,0:T(8,128)(2,1)S(1)}, bf16[16,16,384]{2,1,0:T(8,128)(2,1)S(1)}, u32[]{:S(2)}, u32[]{:S(2)}) collective-permute-start(bf16[16,16,384]{2,1,0:T(8,128)(2,1)S(1)} %get-tuple-element.76), channel_id=1, source_target_pairs={{0,64},{16,80},{32,96},{48,112},{64,128},{80,144},{96,160},{112,17... | collective-permute-start | bytes 589832 | tf_op jit(solution)/shard_map/ppermute | solution.py:427
  113.1 23.9 %copy-start.3 = (bf16[16,16,384]{2,1,0:T(8,128)(2,1)}, bf16[16,16,384]{2,1,0:T(8,128)(2,1)S(1)}, u32[]{:S(2)}) copy-start(bf16[16,16,384]{2,1,0:T(8,128)(2,1)S(1)} %collective-permute-done.12.refs_7_) | copy-start | bytes 589828
  113.1 19.4 %collective-permute-start.5 = (bf16[16,16,384]{2,1,0:T(8,128)(2,1)S(1)}, bf16[16,16,384]{2,1,0:T(8,128)(2,1)S(1)}, u32[]{:S(2)}, u32[]{:S(2)}) collective-permute-start(bf16[16,16,384]{2,1,0:T(8,128)(2,1)S(1)} %get-tuple-element.77), channel_id=1, source_target_pairs={{0,128},{16,144},{32,160},{48,176},{64,192},{80,208},{96,224},{112... | collective-permute-start | bytes 589832 | tf_op jit(solution)/shard_map/ppermute | solution.py:427
  122.3 14.6 %copy-start.4 = (bf16[16,16,384]{2,1,0:T(8,128)(2,1)}, bf16[16,16,384]{2,1,0:T(8,128)(2,1)S(1)}, u32[]{:S(2)}) copy-start(bf16[16,16,384]{2,1,0:T(8,128)(2,1)S(1)} %collective-permute-done.13.refs_8_) | copy-start | bytes 589828
  122.3 12.2 %collective-permute-start.4 = (bf16[16,16,384]{2,1,0:T(8,128)(2,1)S(1)}, bf16[16,16,384]{2,1,0:T(8,128)(2,1)S(1)}, u32[]{:S(2)}, u32[]{:S(2)}) collective-permute-start(bf16[16,16,384]{2,1,0:T(8,128)(2,1)S(1)} %get-tuple-element.78), channel_id=1, source_target_pairs={{0,192},{16,208},{32,224},{48,240},{64,0},{80,16},{96,32},{112,48}... | collective-permute-start | bytes 589832 | tf_op jit(solution)/shard_map/ppermute | solution.py:427
  122.9 14.1 %copy-start.5 = (bf16[16,16,384]{2,1,0:T(8,128)(2,1)}, bf16[16,16,384]{2,1,0:T(8,128)(2,1)S(1)}, u32[]{:S(2)}) copy-start(bf16[16,16,384]{2,1,0:T(8,128)(2,1)S(1)} %collective-permute-done.14.refs_9_) | copy-start | bytes 589828
  122.9 14.2 %collective-permute-start.7 = (bf16[16,16,384]{2,1,0:T(8,128)(2,1)}, bf16[16,16,384]{2,1,0:T(8,128)(2,1)}, u32[]{:S(2)}, u32[]{:S(2)}) collective-permute-start(bf16[16,16,384]{2,1,0:T(8,128)(2,1)} %get-tuple-element.52), channel_id=1, source_target_pairs={{0,2},{1,3},{2,4},{3,5},{4,6},{5,7},{6,8},{7,9},{8,10},{9,11},{10,... | collective-permute-start | bytes 589832 | tf_op jit(solution)/shard_map/ppermute | solution.py:448
  126.7 10.3 %copy-start.6 = (bf16[16,16,384]{2,1,0:T(8,128)(2,1)}, bf16[16,16,384]{2,1,0:T(8,128)(2,1)S(1)}, u32[]{:S(2)}) copy-start(bf16[16,16,384]{2,1,0:T(8,128)(2,1)S(1)} %collective-permute-done.6.refs_1_) | copy-start | bytes 589828
  126.7 16.8 %collective-permute-start.8 = (bf16[16,16,384]{2,1,0:T(8,128)(2,1)}, bf16[16,16,384]{2,1,0:T(8,128)(2,1)}, u32[]{:S(2)}, u32[]{:S(2)}) collective-permute-start(bf16[16,16,384]{2,1,0:T(8,128)(2,1)} %get-tuple-element.53), channel_id=1, source_target_pairs={{0,3},{1,4},{2,5},{3,6},{4,7},{5,8},{6,9},{7,10},{8,11},{9,12},{10... | collective-permute-start | bytes 589832 | tf_op jit(solution)/shard_map/ppermute | solution.py:448
  131.3 14.5 %collective-permute-start.9 = (bf16[16,16,384]{2,1,0:T(8,128)(2,1)}, bf16[16,16,384]{2,1,0:T(8,128)(2,1)}, u32[]{:S(2)}, u32[]{:S(2)}) collective-permute-start(bf16[16,16,384]{2,1,0:T(8,128)(2,1)} %get-tuple-element.54), channel_id=1, source_target_pairs={{0,4},{1,5},{2,6},{3,7},{4,8},{5,9},{6,10},{7,11},{8,12},{9,13},{1... | collective-permute-start | bytes 589832 | tf_op jit(solution)/shard_map/ppermute | solution.py:448
  132.4 31.0 %collective-permute-start.10 = (bf16[16,16,384]{2,1,0:T(8,128)(2,1)}, bf16[16,16,384]{2,1,0:T(8,128)(2,1)}, u32[]{:S(2)}, u32[]{:S(2)}) collective-permute-start(bf16[16,16,384]{2,1,0:T(8,128)(2,1)} %get-tuple-element.55), channel_id=1, source_target_pairs={{0,5},{1,6},{2,7},{3,8},{4,9},{5,10},{6,11},{7,12},{8,13},{9,14},{... | collective-permute-start | bytes 589832 | tf_op jit(solution)/shard_map/ppermute | solution.py:448
  134.6 28.9 %collective-permute-start.15 = (bf16[16,16,384]{2,1,0:T(8,128)(2,1)}, bf16[16,16,384]{2,1,0:T(8,128)(2,1)}, u32[]{:S(2)}, u32[]{:S(2)}) collective-permute-start(bf16[16,16,384]{2,1,0:T(8,128)(2,1)} %get-tuple-element.60), channel_id=1, source_target_pairs={{0,10},{1,11},{2,12},{3,13},{4,14},{5,15},{6,0},{7,1},{8,2},{9,3},... | collective-permute-start | bytes 589832 | tf_op jit(solution)/shard_map/ppermute | solution.py:448
  137.1 26.4 %copy-start.1 = (bf16[16,16,16,384]{3,2,1,0:T(8,128)(2,1)}, bf16[16,16,16,384]{3,2,1,0:T(8,128)(2,1)S(1)}, u32[]{:S(2)}) copy-start(bf16[16,16,16,384]{3,2,1,0:T(8,128)(2,1)S(1)} %all-to-all-done.received) | copy-start | bytes 9437188
  137.1 45.3 %collective-permute-start.16 = (bf16[16,16,384]{2,1,0:T(8,128)(2,1)}, bf16[16,16,384]{2,1,0:T(8,128)(2,1)}, u32[]{:S(2)}, u32[]{:S(2)}) collective-permute-start(bf16[16,16,384]{2,1,0:T(8,128)(2,1)} %get-tuple-element.61), channel_id=1, source_target_pairs={{0,11},{1,12},{2,13},{3,14},{4,15},{5,0},{6,1},{7,2},{8,3},{9,4},{... | collective-permute-start | bytes 589832 | tf_op jit(solution)/shard_map/ppermute | solution.py:448
  143.5 38.9 %collective-permute-start.17 = (bf16[16,16,384]{2,1,0:T(8,128)(2,1)}, bf16[16,16,384]{2,1,0:T(8,128)(2,1)}, u32[]{:S(2)}, u32[]{:S(2)}) collective-permute-start(bf16[16,16,384]{2,1,0:T(8,128)(2,1)} %get-tuple-element.62), channel_id=1, source_target_pairs={{0,12},{1,13},{2,14},{3,15},{4,0},{5,1},{6,2},{7,3},{8,4},{9,5},{1... | collective-permute-start | bytes 589832 | tf_op jit(solution)/shard_map/ppermute | solution.py:448
  145.8 36.6 %collective-permute-start.18 = (bf16[16,16,384]{2,1,0:T(8,128)(2,1)}, bf16[16,16,384]{2,1,0:T(8,128)(2,1)}, u32[]{:S(2)}, u32[]{:S(2)}) collective-permute-start(bf16[16,16,384]{2,1,0:T(8,128)(2,1)} %get-tuple-element.63), channel_id=1, source_target_pairs={{0,13},{1,14},{2,15},{3,0},{4,1},{5,2},{6,3},{7,4},{8,5},{9,6},{10... | collective-permute-start | bytes 589832 | tf_op jit(solution)/shard_map/ppermute | solution.py:448
  163.4 19.0 %collective-permute-start.19 = (bf16[16,16,384]{2,1,0:T(8,128)(2,1)}, bf16[16,16,384]{2,1,0:T(8,128)(2,1)}, u32[]{:S(2)}, u32[]{:S(2)}) collective-permute-start(bf16[16,16,384]{2,1,0:T(8,128)(2,1)} %get-tuple-element.64), channel_id=1, source_target_pairs={{0,14},{1,15},{2,0},{3,1},{4,2},{5,3},{6,4},{7,5},{8,6},{9,7},{10,... | collective-permute-start | bytes 589832 | tf_op jit(solution)/shard_map/ppermute | solution.py:448
  163.4 19.0 %collective-permute-start.20 = (bf16[16,16,384]{2,1,0:T(8,128)(2,1)}, bf16[16,16,384]{2,1,0:T(8,128)(2,1)}, u32[]{:S(2)}, u32[]{:S(2)}) collective-permute-start(bf16[16,16,384]{2,1,0:T(8,128)(2,1)} %get-tuple-element.65), channel_id=1, source_target_pairs={{0,15},{1,0},{2,1},{3,2},{4,3},{5,4},{6,5},{7,6},{8,7},{9,8},{10,9... | collective-permute-start | bytes 589832 | tf_op jit(solution)/shard_map/ppermute | solution.py:448
  202.3 13.3 %collective-permute-start.21 = (bf16[4,8,16,384]{3,2,1,0:T(8,128)(2,1)}, bf16[4,8,16,384]{3,2,1,0:T(8,128)(2,1)S(1)}, u32[]{:S(2)}, u32[]{:S(2)}) collective-permute-start(bf16[4,8,16,384]{3,2,1,0:T(8,128)(2,1)} %get-tuple-element.68), channel_id=1, source_target_pairs={{0,16},{16,32},{32,48},{48,0},{64,80},{80,96},{96,112},{112,64},{1... | collective-permute-start | bytes 1179656 | tf_op jit(solution)/shard_map/ppermute | solution.py:427
  203.9 19.8 %collective-permute-start.22 = (bf16[4,8,16,384]{3,2,1,0:T(8,128)(2,1)}, bf16[4,8,16,384]{3,2,1,0:T(8,128)(2,1)S(1)}, u32[]{:S(2)}, u32[]{:S(2)}) collective-permute-start(bf16[4,8,16,384]{3,2,1,0:T(8,128)(2,1)} %get-tuple-element.69), channel_id=1, source_target_pairs={{0,48},{16,0},{32,16},{48,32},{64,112},{80,64},{96,80},{112,96},{1... | collective-permute-start | bytes 1179656 | tf_op jit(solution)/shard_map/ppermute | solution.py:427
  205.7 19.5 %collective-permute-start.23 = (bf16[4,8,16,384]{3,2,1,0:T(8,128)(2,1)}, bf16[4,8,16,384]{3,2,1,0:T(8,128)(2,1)S(1)}, u32[]{:S(2)}, u32[]{:S(2)}) collective-permute-start(bf16[4,8,16,384]{3,2,1,0:T(8,128)(2,1)} %get-tuple-element.70), channel_id=1, source_target_pairs={{0,32},{16,48},{32,0},{48,16},{64,96},{80,112},{96,64},{112,80},{1... | collective-permute-start | bytes 1179656 | tf_op jit(solution)/shard_map/ppermute | solution.py:427
  207.6 22.0 %collective-permute-start.27 = (bf16[4,8,16,384]{3,2,1,0:T(8,128)(2,1)}, bf16[4,8,16,384]{3,2,1,0:T(8,128)(2,1)S(1)}, u32[]{:S(2)}, u32[]{:S(2)}) collective-permute-start(bf16[4,8,16,384]{3,2,1,0:T(8,128)(2,1)} %get-tuple-element.72), channel_id=1, source_target_pairs={{0,64},{16,80},{32,96},{48,112},{64,128},{80,144},{96,160},{112,17... | collective-permute-start | bytes 1179656 | tf_op jit(solution)/shard_map/ppermute | solution.py:427
  208.5 21.3 %collective-permute-start.28 = (bf16[4,8,16,384]{3,2,1,0:T(8,128)(2,1)}, bf16[4,8,16,384]{3,2,1,0:T(8,128)(2,1)S(1)}, u32[]{:S(2)}, u32[]{:S(2)}) collective-permute-start(bf16[4,8,16,384]{3,2,1,0:T(8,128)(2,1)} %get-tuple-element.73), channel_id=1, source_target_pairs={{0,192},{16,208},{32,224},{48,240},{64,0},{80,16},{96,32},{112,48}... | collective-permute-start | bytes 1179656 | tf_op jit(solution)/shard_map/ppermute | solution.py:427
  215.6 14.3 %collective-permute-start.29 = (bf16[4,8,16,384]{3,2,1,0:T(8,128)(2,1)}, bf16[4,8,16,384]{3,2,1,0:T(8,128)(2,1)S(1)}, u32[]{:S(2)}, u32[]{:S(2)}) collective-permute-start(bf16[4,8,16,384]{3,2,1,0:T(8,128)(2,1)} %get-tuple-element.74), channel_id=1, source_target_pairs={{0,128},{16,144},{32,160},{48,176},{64,192},{80,208},{96,224},{112... | collective-permute-start | bytes 1179656 | tf_op jit(solution)/shard_map/ppermute | solution.py:427
  226.4 13.7 %collective-permute-start.24 = (bf16[8,16,384]{2,1,0:T(8,128)(2,1)S(1)}, bf16[8,16,384]{2,1,0:T(8,128)(2,1)S(1)}, u32[]{:S(2)}, u32[]{:S(2)}) collective-permute-start(bf16[8,16,384]{2,1,0:T(8,128)(2,1)S(1)} %get-tuple-element.79), channel_id=1, source_target_pairs={{0,64},{16,80},{32,96},{48,112},{64,128},{80,144},{96,160},{112,17... | collective-permute-start | bytes 294920 | tf_op jit(solution)/shard_map/ppermute | solution.py:427
  227.6 15.0 %collective-permute-start.26 = (bf16[8,16,384]{2,1,0:T(8,128)(2,1)S(1)}, bf16[8,16,384]{2,1,0:T(8,128)(2,1)S(1)}, u32[]{:S(2)}, u32[]{:S(2)}) collective-permute-start(bf16[8,16,384]{2,1,0:T(8,128)(2,1)S(1)} %get-tuple-element.80), channel_id=1, source_target_pairs={{0,128},{16,144},{32,160},{48,176},{64,192},{80,208},{96,224},{112... | collective-permute-start | bytes 294920 | tf_op jit(solution)/shard_map/ppermute | solution.py:427
  229.6 13.1 %collective-permute-start.25 = (bf16[8,16,384]{2,1,0:T(8,128)(2,1)S(1)}, bf16[8,16,384]{2,1,0:T(8,128)(2,1)S(1)}, u32[]{:S(2)}, u32[]{:S(2)}) collective-permute-start(bf16[8,16,384]{2,1,0:T(8,128)(2,1)S(1)} %get-tuple-element.81), channel_id=1, source_target_pairs={{0,192},{16,208},{32,224},{48,240},{64,0},{80,16},{96,32},{112,48}... | collective-permute-start | bytes 294920 | tf_op jit(solution)/shard_map/ppermute | solution.py:427
  231.1 11.7 %collective-permute-start.30 = (bf16[8,16,384]{2,1,0:T(8,128)(2,1)S(1)}, bf16[8,16,384]{2,1,0:T(8,128)(2,1)S(1)}, u32[]{:S(2)}, u32[]{:S(2)}) collective-permute-start(bf16[8,16,384]{2,1,0:T(8,128)(2,1)S(1)} %get-tuple-element.82), channel_id=1, source_target_pairs={{0,16},{16,32},{32,48},{48,0},{64,80},{80,96},{96,112},{112,64},{1... | collective-permute-start | bytes 294920 | tf_op jit(solution)/shard_map/ppermute | solution.py:427
  232.7 11.0 %collective-permute-start.32 = (bf16[8,16,384]{2,1,0:T(8,128)(2,1)S(1)}, bf16[8,16,384]{2,1,0:T(8,128)(2,1)S(1)}, u32[]{:S(2)}, u32[]{:S(2)}) collective-permute-start(bf16[8,16,384]{2,1,0:T(8,128)(2,1)S(1)} %get-tuple-element.83), channel_id=1, source_target_pairs={{0,32},{16,48},{32,0},{48,16},{64,96},{80,112},{96,64},{112,80},{1... | collective-permute-start | bytes 294920 | tf_op jit(solution)/shard_map/ppermute | solution.py:427
  240.1 4.7 %collective-permute-start.31 = (bf16[8,16,384]{2,1,0:T(8,128)(2,1)S(1)}, bf16[8,16,384]{2,1,0:T(8,128)(2,1)S(1)}, u32[]{:S(2)}, u32[]{:S(2)}) collective-permute-start(bf16[8,16,384]{2,1,0:T(8,128)(2,1)S(1)} %get-tuple-element.84), channel_id=1, source_target_pairs={{0,48},{16,0},{32,16},{48,32},{64,112},{80,64},{96,80},{112,96},{1... | collective-permute-start | bytes 294920 | tf_op jit(solution)/shard_map/ppermute | solution.py:427
  276.3 75.5 %all-to-all-start.1 = ((bf16[16,16,16,384]{3,2,1,0:T(8,128)(2,1)}), bf16[16,16,16,384]{3,2,1,0:T(8,128)(2,1)S(1)}, u32[]{:S(2)}, u32[]{:S(2)}) async-start(bf16[16,16,16,384]{3,2,1,0:T(8,128)(2,1)} %get-tuple-element.49), calls=%async_computation.1 | async-start | bytes 6291456 | tf_op jit(solution)/shard_map/all_to_all | solution.py:452
  351.8 1.6 copy-start
